TPU v7x, 512 devices: a whole 4x8x8 slice. The times are simulated.
512 devices in a mesh: dp: 32 (over z, y_hi), tensor: 16 (over x, y_lo, core).
Axes of the slice: x: 4, y: 8 (y_hi: 4, y_lo: 2; y = y_hi * 2 + y_lo), z: 8, core: 2. Of those that a mesh axis runs over, the one named last changes fastest.
Arguments:
- hidden: bfloat16 [16384, 7168], P('dp', 'tensor'), may hold values from -6 to 6
- w_down: bfloat16 [7168, 576], P('tensor'), may hold values from -0.0625 to 0.0625
- norm_gain: float32 [512], replicated, may hold values from 0.25 to 1.75
- w_up: bfloat16 [512, 32768], P('dp', 'tensor'), may hold values from -0.25 to 0.25
- kv_grad: bfloat16 [16384, 32768], P('dp', 'tensor'), may hold values from -6 to 6
- rope_grad: bfloat16 [16384, 64], P('dp'), may hold values from -6 to 6
Outputs:
- hidden_grad: bfloat16 [16384, 7168], P('dp', 'tensor')
- down_grad: bfloat16 [7168, 576], P('tensor')
- gain_grad: float32 [512], replicated
- up_grad: bfloat16 [512, 32768], P('dp', 'tensor')
All inputs are finite; a program needn't handle non-finite values.
Results may differ from a plain program's by a relative error of at most 0.005.
Values may be sent and summed in bfloat16 or wider, within the bound.
No kernel may reach another device: no remote copies, remote signals or barrier semaphores. Data moves between devices by JAX's collectives and lax.ppermute only.
A program may use at most 64 MiB of HBM per device.

v0:
```python
import jax
import jax.numpy as jnp
from jax import lax
from jax.sharding import PartitionSpec as P

MB = 256
MICROS = 2


def norm_back(projected, latent_grad, norm_gain, lat_width):
    inv_rms = lax.rsqrt(jnp.mean(projected * projected, axis=1, keepdims=True) + 1e-06)
    latent = (projected * inv_rms * norm_gain).astype(jnp.bfloat16)
    gain_share = jnp.sum(latent_grad * projected * inv_rms, axis=0)
    scaled = norm_gain * latent_grad
    proj_grad = (
        inv_rms * scaled
        - projected
        * inv_rms
        * inv_rms
        * inv_rms
        * jnp.sum(scaled * projected, axis=1, keepdims=True)
        / lat_width
    ).astype(jnp.bfloat16)
    return (latent, proj_grad, gain_share)


def shards(hidden, w_down, norm_gain, w_up, kv_grad, rope_grad):
    lat_width = norm_gain.shape[0]
    latent_grad_all = lax.dot_general(
        kv_grad,
        lax.all_gather(w_up, "dp", axis=0, tiled=True),
        (((1,), (1,)), ((), ())),
        preferred_element_type=jnp.float32,
    )
    up_running = jnp.zeros((lat_width, kv_grad.shape[1]), jnp.float32)
    down_running = jnp.zeros((w_down.shape[0], w_down.shape[1]), jnp.float32)
    gain_running = jnp.zeros((lat_width,), jnp.float32)
    input_grads = []
    for micro_index in range(MICROS):
        row_range = slice(micro_index * MB, (micro_index + 1) * MB)
        hidden_rows = hidden[row_range]
        cot_rows = kv_grad[row_range]
        proj_partial = jnp.dot(
            hidden_rows, w_down[:, :lat_width], preferred_element_type=jnp.float32
        )
        proj_full, lgrad_full = lax.psum((proj_partial, latent_grad_all[row_range]), "tensor")
        latent, proj_grad, gain_share = norm_back(proj_full, lgrad_full, norm_gain, lat_width)
        gain_running = gain_running + gain_share
        up_running = up_running + lax.dot_general(
            latent, cot_rows, (((0,), (0,)), ((), ())), preferred_element_type=jnp.float32
        )
        joint_grad = jnp.concatenate([proj_grad, rope_grad[row_range]], axis=1)
        down_running = down_running + lax.dot_general(
            hidden_rows, joint_grad, (((0,), (0,)), ((), ())), preferred_element_type=jnp.float32
        )
        input_grads.append(
            lax.dot_general(
                joint_grad, w_down, (((1,), (1,)), ((), ())), preferred_element_type=jnp.float32
            ).astype(jnp.bfloat16)
        )
    hidden_grad = jnp.concatenate(input_grads, axis=0)
    gain_grad = lax.psum(gain_running, "dp")
    up_grad = lax.psum_scatter(up_running, "dp", scatter_dimension=0, tiled=True).astype(
        jnp.bfloat16
    )
    down_grad = lax.psum(down_running, "dp").astype(jnp.bfloat16)
    return (hidden_grad, down_grad, gain_grad, up_grad)


def solution(mesh):
    placed = (
        P("dp", "tensor"),
        P("tensor", None),
        P(),
        P("dp", "tensor"),
        P("dp", "tensor"),
        P("dp", None),
    )
    return jax.shard_map(
        shards,
        mesh=mesh,
        in_specs=placed,
        out_specs=(P("dp", "tensor"), P("tensor", None), P(), P("dp", "tensor")),
        check_vma=False,
    )
```

profile of v0, /device:TPU:2, one launch (start us, length us, event | category | flops | bytes accessed | tf_op | source)
XLA Modules:
  0.0 486.4 jit_solution(1724037319380611540)
XLA Ops:
  7.2 0.0 all-gather.2.cloned.1.call-start
  7.2 0.7 all-gather.2.cloned.1.call-update
  7.9 0.0 all-reduce.5.cloned.1.call-start
  8.0 2.3 fusion.4
  10.2 2.3 fusion.6
  12.5 89.5 %all-gather.2.cloned.1.call-done = bf16[512,2048]{1,0:T(8,128)(2,1)} async-done(((bf16[16,2048]{1,0:T(8,128)(2,1)}), bf16[512,2048]{1,0:T(8,128)(2,1)}) %all-gather.2.cloned.1.call-update) | async-done | bytes 2097168 | tf_op jit(solution)/shard_map/all_gather | solution.py:31
  102.0 2.9 fusion.23
  104.9 1.1 fusion.21
  105.9 0.0 all-reduce.5.cloned.1.call-update
  105.9 0.0 reduce-scatter.2.cloned.1.call-start
  106.0 127.0 %all-reduce.5.cloned.1.call-done = (f32[256,512]{1,0:T(8,128)}, f32[256,512]{1,0:T(8,128)}, f32[256,512]{1,0:T(8,128)}, f32[256,512]{1,0:T(8,128)}) async-done(((f32[256,512]{1,0:T(8,128)}, f32[256,512]{1,0:T(8,128)}, f32[256,512]{1,0:T(8,128)}, f32[256,512]{1,0:T(8,128)}), (f32[256,512]{1,0:T(8,128)}, f32[256,512]{1,0:T(8,128)}, f32[256,512]{1,0:T(8,128)}, ...) | async-done | bytes 2097168 | tf_op jit(solution)/shard_map/psum | solution.py:46
  233.0 1.3 multiply_reduce_fusion.3
  234.4 1.9 fusion.2
  236.3 2.8 convolution_add_fusion
  239.1 0.0 reduce-scatter.2.cloned.1.call-update
  239.1 0.8 copy-done.8
  239.9 0.1 copy.12
  240.1 0.1 copy.13
  240.2 0.1 copy-done.2
  240.3 0.2 copy-done.3
  240.5 0.4 multiply_reduce_fusion.1
  240.9 0.4 subtract_convert_fusion.1
  241.3 0.2 copy-done.5
  241.5 0.3 fusion.12
  241.9 0.3 fusion
  242.2 0.4 copy-done.6
  242.6 0.4 convolution_convert_fusion.1
  243.0 0.4 convolution_convert_fusion
  243.3 0.8 pad_maximum_fusion
  244.1 184.4 %all-reduce.6 = (bf16[448,576]{1,0:T(8,128)(2,1)}, f32[512]{0:T(512)}) all-reduce(f32[448,576]{1,0:T(8,128)S(1)} %fusion, f32[512]{0:T(512)S(1)} %add.46), channel_id=1, replica_groups=mesh['dp'=32,'tensor'=16] {'dp'}, use_global_device_ids=true, to_apply=%region_8.0 | all-reduce | flops 258560 | bytes 1552384 | tf_op jit(solution)/shard_map/psum | solution.py:66
  428.5 49.8 %reduce-scatter.2.cloned.1.call-done = f32[16,2048]{1,0:T(8,128)} async-done(((f32[512,2048]{1,0:T(8,128)}), f32[16,2048]{1,0:T(8,128)}) %reduce-scatter.2.cloned.1.call-update) | async-done | bytes 131088 | tf_op jit(solution)/shard_map/reduce_scatter | solution.py:63
  478.3 1.5 convert_element_type.31
  (17 shorter events, 0.0 us)
Async XLA Ops:
  7.2 94.8 %copy-start.4 = (bf16[512,2048]{1,0:T(8,128)(2,1)S(1)}, bf16[512,2048]{1,0:T(8,128)(2,1)}, u32[]{:S(2)}) copy-start(bf16[512,2048]{1,0:T(8,128)(2,1)} %param.10) | copy-start | bytes 6291460
  7.2 94.8 %all-gather.2.cloned.1.call-start = ((), (), s32[]{:S(2)}) async-start(), calls=%async_computation.1 | async-start | bytes 2162688 | tf_op jit(solution)/shard_map/all_gather | solution.py:31
  7.9 225.1 %all-reduce.5.cloned.1.call-start = ((), (), s32[]{:S(2)}) async-start(), calls=%async_computation.3 | async-start | bytes 4194304 | tf_op jit(solution)/shard_map/psum | solution.py:46
  105.9 128.4 %copy-start.7 = (f32[512]{0:T(512)S(1)}, f32[512]{0:T(512)}, u32[]{:S(2)}) copy-start(f32[512]{0:T(512)} %param.8) | copy-start | bytes 6148
  105.9 372.4 %reduce-scatter.2.cloned.1.call-start = ((), (), s32[]{:S(2)}) async-start(), calls=%async_computation.2 | async-start | bytes 4325376 | tf_op jit(solution)/shard_map/reduce_scatter | solution.py:63
  234.4 1.9 copy-start.1
  239.1 0.8 copy-start.8
  239.1 1.1 copy-start
  239.1 1.2 copy-start.2
  239.1 1.4 copy-start.3
  240.5 1.0 copy-start.5
  241.5 1.1 copy-start.6
Sparse Core Ops, SparseCore 0:
  11.2 90.7 all-gather.1
  106.1 126.8 all-reduce.4
  239.3 239.0 reduce-scatter.1
where the time goes:
time: 487 us; the launch traced here: 486 us
  waiting for transfers between devices  267 us (55%)
  blocking collectives  184 us (38%)
  between operations  13.9 us (3%)
  matrix products  13.6 us (3%)
    psum x1, blocking collectives, shards(): down_grad = lax.psum(down_running, 'dp').astype(jnp.bfloat16)  184 us
    psum x1, waiting for transfers between devices, shards(): lax.psum((proj_partial, latent_grad_all[row_range]), 'tensor')  127 us
    all_gather x1, waiting for transfers between devices, shards(): lax.all_gather(w_up, 'dp', axis=0, tiled=True)  89.5 us
    reduce_scatter x1, waiting for transfers between devices, shards(): lax.psum_scatter(up_running, 'dp', scatter_dimension=0, tiled=True)  49.8 us
  transfers between devices with their start and end apart: 3, of which 3 were waited for; matrix products, arithmetic and copies ran while one was open for 2% of the time, Pallas kernels for 0%

commit v1 on v0

v1 whole, which is shorter than its diff:
```python
import jax
import jax.numpy as jnp
from jax import lax
from jax.sharding import Mesh
from jax.sharding import PartitionSpec as P

ALL = ("z", "yh", "x", "yl", "core")
DP = ("z", "yh")
TENSOR = ("x", "yl", "core")
GAIN_ROWS = 8
LANES = 512


def dot(a, b, dims):
    return lax.dot_general(a, b, (dims, ((), ())), preferred_element_type=jnp.float32)


def two_halves(value):
    high = value.astype(jnp.bfloat16)
    low = (value - high.astype(jnp.float32)).astype(jnp.bfloat16)
    return (high, low)


def scatter_sum(partial, axes, parts):
    pieces = partial.reshape((parts, -1) + partial.shape[1:])
    arrived = lax.all_to_all(pieces, axes, 0, 0, tiled=True)
    return jnp.sum(arrived.astype(jnp.float32), axis=0)


def spread(piece, axes, parts):
    copies = jnp.broadcast_to(piece[None], (parts,) + piece.shape)
    return lax.all_to_all(copies, axes, 0, 0, tiled=True)


def after(value, earlier):
    return lax.optimization_barrier((value, earlier))[0]


def with_gain(down, gain):
    high, low = two_halves(gain)
    lanes = jnp.stack([high, low], axis=-2)
    rows = [(0, 0)] * (lanes.ndim - 2) + [(0, down.shape[-2] - 2), (0, 0)]
    return jnp.concatenate([down.astype(jnp.bfloat16), jnp.pad(lanes, rows)], axis=-1)


def parted(both, width):
    lanes = both[..., :2, width:].astype(jnp.float32)
    return both[..., :width], lanes[..., 0, :] + lanes[..., 1, :]


def body(sizes, hidden, w_down, norm_gain, w_up, kv_grad, rope_grad):
    n_z, n_yh, n_t = sizes
    lat = norm_gain.shape[0]
    width = w_down.shape[1]
    w_up_near = spread(w_up, "yh", n_yh).reshape(-1, w_up.shape[1])
    w_up_all = lax.all_gather(w_up_near, "z", axis=0, tiled=True)

    projected = scatter_sum(
        dot(hidden, w_down[:, :lat], ((1,), (0,))), TENSOR, n_t
    )
    inv_rms = lax.rsqrt(jnp.mean(projected * projected, axis=1, keepdims=True) + 1e-06)
    latent = (projected * inv_rms * norm_gain).astype(jnp.bfloat16)
    latent_all = spread(latent, TENSOR, n_t).reshape(-1, lat)

    up_part = dot(latent_all, kv_grad, ((0,), (0,))).astype(jnp.bfloat16)
    up_sum = lax.psum_scatter(up_part, "z", scatter_dimension=0, tiled=True)
    grad_part = dot(kv_grad, after(w_up_all, up_part), ((1,), (1,)))
    latent_grad = scatter_sum(grad_part.astype(jnp.bfloat16), TENSOR, n_t)
    gain_share = jnp.sum(latent_grad * projected * inv_rms, axis=0)
    scaled = norm_gain * latent_grad
    proj_grad = (
        inv_rms * scaled
        - projected
        * inv_rms
        * inv_rms
        * inv_rms
        * jnp.sum(scaled * projected, axis=1, keepdims=True)
        / lat
    ).astype(jnp.bfloat16)
    high, low = two_halves(gain_share)
    fill = jnp.zeros((GAIN_ROWS - 2, lat), jnp.bfloat16)
    joined = spread(
        jnp.concatenate([proj_grad, high[None], low[None], fill], axis=0), TENSOR, n_t
    )
    rows = proj_grad.shape[0]
    joint_grad = jnp.concatenate([joined[:, :rows].reshape(-1, lat), rope_grad], axis=1)
    gain_group = jnp.sum(joined[:, rows : rows + 2].astype(jnp.float32), axis=(0, 1))

    hidden_grad = dot(joint_grad, w_down, ((1,), (1,))).astype(jnp.bfloat16)

    down_part = dot(hidden, joint_grad, ((0,), (0,)))
    packed = with_gain(down_part.reshape(n_z, -1, width), gain_group.reshape(n_z, -1))
    arrived = lax.all_to_all(packed, "z", 0, 0, tiled=True).astype(jnp.float32)
    down_sum, gain_sum = parted(jnp.sum(arrived, axis=0), width)
    packed = with_gain(down_sum, gain_sum)
    near = packed.shape[0]
    up_rows = up_sum.shape[0] // n_yh
    up_cut = up_sum.reshape(n_yh, up_rows, -1, LANES).transpose(0, 2, 1, 3)
    up_cut = up_cut.reshape(n_yh, -1, LANES)
    up_cut = jnp.pad(up_cut, [(0, 0), (0, 0), (0, packed.shape[1] - LANES)])
    copies = jnp.broadcast_to(packed[None], (n_yh,) + packed.shape)
    both = jnp.concatenate([copies, up_cut], axis=1)
    arrived = lax.all_to_all(both, "yh", 0, 0, tiled=True)
    up_grad = jnp.sum(arrived[:, near:, :LANES].astype(jnp.float32), axis=0)
    up_grad = up_grad.reshape(-1, up_rows, LANES).transpose(1, 0, 2)
    up_grad = up_grad.reshape(up_rows, -1).astype(jnp.bfloat16)
    down_sum, gain_sum = parted(
        jnp.sum(arrived[:, :near].astype(jnp.float32), axis=0), width
    )
    arrived = spread(with_gain(down_sum, gain_sum), "z", n_z)
    down_grad, gain_grad = parted(arrived, width)
    return (hidden_grad, down_grad.reshape(-1, width), gain_grad.reshape(-1), up_grad)


def solution(mesh):
    n_z, n_yh, n_x, n_yl, n_core = 8, 4, 4, 2, 2
    fine = Mesh(mesh.devices.reshape(n_z, n_yh, n_x, n_yl, n_core), ALL)

    def shards(*args):
        return body((n_z, n_yh, n_x * n_yl * n_core), *args)

    return jax.shard_map(
        shards,
        mesh=fine,
        in_specs=(
            P(DP, TENSOR),
            P(TENSOR, None),
            P(),
            P(DP, TENSOR),
            P(DP, TENSOR),
            P(DP, None),
        ),
        out_specs=(P(DP, TENSOR), P(TENSOR, None), P(), P(DP, TENSOR)),
        check_vma=False,
    )
```

time: 487 us -> 203 us (0.42)
  the two profiles are of different devices: /device:TPU:2 before, /device:TPU:23 now
where the time goes in v1:
time: 203 us; the launch traced here: 202 us
  waiting for transfers between devices  91.1 us (45%)
  starting transfers between devices  44.6 us (22%)
  blocking collectives  30.4 us (15%)
  between operations  14.2 us (7%)
  matrix products  12 us (6%)
  local copies, waits for them, and re-layouts  7.94 us (4%)
  other arithmetic  2.25 us (1%)
    all_to_all x3, waiting for transfers between devices, spread(): return lax.all_to_all(copies, axes, 0, 0, tiled=True)  32.6 us
    all_to_all x3, starting transfers between devices, spread(): return lax.all_to_all(copies, axes, 0, 0, tiled=True)  25.3 us
    all_to_all x2, waiting for transfers between devices, scatter_sum(): arrived = lax.all_to_all(pieces, axes, 0, 0, tiled=True)  19.9 us
    reduce_scatter x1, waiting for transfers between devices, body(): up_sum = lax.psum_scatter(up_part, 'z', scatter_dimension=0, tiled=True)  18.2 us
    all_to_all x1, blocking collectives, body(): arrived = lax.all_to_all(both, 'yh', 0, 0, tiled=True)  17.1 us
    all_gather x1, waiting for transfers between devices, body(): w_up_all = lax.all_gather(w_up_near, 'z', axis=0, tiled=True)  15.9 us
    all_to_all x2, starting transfers between devices, scatter_sum(): arrived = lax.all_to_all(pieces, axes, 0, 0, tiled=True)  15.4 us
    all_to_all x1, blocking collectives, spread(): return lax.all_to_all(copies, axes, 0, 0, tiled=True)  13.3 us
  transfers between devices with their start and end apart: 8, of which 8 were waited for; matrix products, arithmetic and copies ran while one was open for 6% of the time, Pallas kernels for 0%

profile of v1, /device:TPU:23, one launch (start us, length us, event | category | flops | bytes accessed | tf_op | source)
XLA Modules:
  0.0 202.4 jit_solution(13560294213130005437)
XLA Ops:
  7.2 1.7 broadcast_in_dim.12
  8.9 6.9 %all-to-all-start.1 = ((bf16[4,16,2048]{2,1,0:T(8,128)(2,1)}), bf16[4,16,2048]{2,1,0:T(8,128)(2,1)S(1)}, u32[]{:S(2)}, u32[]{:S(2)}) async-start(bf16[4,16,2048]{2,1,0:T(8,128)(2,1)} %broadcast_in_dim.12), calls=%async_computation.1 | async-start | bytes 524288 | tf_op jit(solution)/shard_map/all_to_all | solution.py:32
  15.8 2.6 %fusion.2 = f32[512,512]{1,0:T(8,128)} fusion(bf16[512,448]{0,1:T(8,128)(2,1)} %param.6, bf16[448,576]{1,0:T(8,128)(2,1)} %param.7), kind=kOutput, calls=%fused_computation.12 | convolution fusion | flops 234881024 | bytes 1966080 | tf_op jit(solution)/shard_map/dot_general | solution.py:15
  18.4 7.4 %all-to-all-done.1 = bf16[4,16,2048]{2,1,0:T(8,128)(2,1)S(1)} async-done(((bf16[4,16,2048]{2,1,0:T(8,128)(2,1)}), bf16[4,16,2048]{2,1,0:T(8,128)(2,1)S(1)}, u32[]{:S(2)}, u32[]{:S(2)}) %all-to-all-start.1) | async-done | bytes 262176 | tf_op jit(solution)/shard_map/all_to_all | solution.py:32
  25.8 5.3 %all-to-all-start = ((f32[16,32,512]{2,1,0:T(8,128)}), f32[16,32,512]{2,1,0:T(8,128)S(1)}, u32[]{:S(2)}, u32[]{:S(2)}) async-start(f32[16,32,512]{2,1,0:T(8,128)} %bitcast.28), calls=%async_computation | async-start | bytes 2097152 | tf_op jit(solution)/shard_map/all_to_all | solution.py:26
  31.1 0.7 all-gather.2.cloned.1.call-update
  31.8 13.0 %all-to-all-done = f32[16,32,512]{2,1,0:T(8,128)S(1)} async-done(((f32[16,32,512]{2,1,0:T(8,128)}), f32[16,32,512]{2,1,0:T(8,128)S(1)}, u32[]{:S(2)}, u32[]{:S(2)}) %all-to-all-start) | async-done | bytes 1048608 | tf_op jit(solution)/shard_map/all_to_all | solution.py:26
  45.2 13.3 %all_to_all.40 = bf16[16,32,512]{2,1,0:T(8,128)(2,1)S(1)} all-to-all(bf16[16,32,512]{2,1,0:T(8,128)(2,1)S(1)} %broadcast_in_dim.13), channel_id=1, replica_groups=mesh['z'=8,'yh'=4,'x'=4,'yl'=2,'core'=2] {'x','yl','core'}, dimensions={0} | all-to-all | bytes 1048576 | tf_op jit(solution)/shard_map/all_to_all | solution.py:32
  58.4 2.6 %convolution_convert_fusion = bf16[512,2048]{1,0:T(8,128)(2,1)} fusion(bf16[512,512]{1,0:T(8,128)(2,1)S(1)} %bitcast.35, bf16[512,2048]{1,0:T(8,128)(2,1)S(1)} %copy-done), kind=kOutput, calls=%fused_computation | convolution fusion | flops 1074790400 | bytes 4718592 | tf_op jit(solution)/shard_map/dot_general | solution.py:15
  61.1 15.9 %all-gather.2.cloned.1.call-done = bf16[512,2048]{1,0:T(8,128)(2,1)} async-done(((bf16[64,2048]{1,0:T(8,128)(2,1)}), bf16[512,2048]{1,0:T(8,128)(2,1)}) %all-gather.2.cloned.1.call-update) | async-done | bytes 2097168 | tf_op jit(solution)/shard_map/all_gather | solution.py:56
  77.0 3.7 %convolution_convert_fusion.2 = bf16[512,512]{0,1:T(8,128)(2,1)} fusion(bf16[512,2048]{1,0:T(8,128)(2,1)} %all-gather.2.cloned.1.call-done, bf16[512,2048]{1,0:T(8,128)(2,1)S(1)} %copy-done), kind=kOutput, calls=%fused_computation.2 | convolution fusion | flops 1074003968 | bytes 4718592 | tf_op jit(solution)/shard_map/dot_general | solution.py:15
  80.6 10.1 %all-to-all-start.3 = ((bf16[16,32,512]{2,1,0:T(8,128)(2,1)}), bf16[16,32,512]{2,1,0:T(8,128)(2,1)S(1)}, u32[]{:S(2)}, u32[]{:S(2)}) async-start(bf16[16,32,512]{2,1,0:T(8,128)(2,1)} %bitcast.4), calls=%async_computation.3 | async-start | bytes 1048576 | tf_op jit(solution)/shard_map/all_to_all | solution.py:26
  90.8 0.7 reduce-scatter.2.cloned.1.call-update
  91.6 6.9 %all-to-all-done.3 = bf16[16,32,512]{2,1,0:T(8,128)(2,1)S(1)} async-done(((bf16[16,32,512]{2,1,0:T(8,128)(2,1)}), bf16[16,32,512]{2,1,0:T(8,128)(2,1)S(1)}, u32[]{:S(2)}, u32[]{:S(2)}) %all-to-all-start.3) | async-done | bytes 524320 | tf_op jit(solution)/shard_map/all_to_all | solution.py:26
  98.9 0.9 broadcast_in_dim.15
  99.8 6.8 %all-to-all-start.4 = ((bf16[16,40,512]{2,1,0:T(8,128)(2,1)}), bf16[16,40,512]{2,1,0:T(8,128)(2,1)S(1)}, u32[]{:S(2)}, u32[]{:S(2)}) async-start(bf16[16,40,512]{2,1,0:T(8,128)(2,1)} %broadcast_in_dim.15), calls=%async_computation.4 | async-start | bytes 1310720 | tf_op jit(solution)/shard_map/all_to_all | solution.py:32
  106.7 9.4 %all-to-all-done.4 = bf16[16,40,512]{2,1,0:T(8,128)(2,1)S(1)} async-done(((bf16[16,40,512]{2,1,0:T(8,128)(2,1)}), bf16[16,40,512]{2,1,0:T(8,128)(2,1)S(1)}, u32[]{:S(2)}, u32[]{:S(2)}) %all-to-all-start.4) | async-done | bytes 655392 | tf_op jit(solution)/shard_map/all_to_all | solution.py:32
  116.4 0.7 copy-done.2
  117.2 0.5 convolution_convert_fusion.1
  117.7 0.9 pad_maximum_fusion.1
  118.6 3.9 %all-to-all-start.5 = ((bf16[8,56,640]{2,1,0:T(8,128)(2,1)}), bf16[8,56,640]{2,1,0:T(8,128)(2,1)S(1)}, u32[]{:S(2)}, u32[]{:S(2)}) async-start(bf16[8,56,640]{2,1,0:T(8,128)(2,1)} %pad_maximum_fusion.1), calls=%async_computation.5 | async-start | bytes 1146880 | tf_op jit(solution)/shard_map/all_to_all | solution.py:93
  122.5 18.2 %reduce-scatter.2.cloned.1.call-done = bf16[64,2048]{1,0:T(8,128)(2,1)} async-done(((bf16[512,2048]{1,0:T(8,128)(2,1)}), bf16[64,2048]{1,0:T(8,128)(2,1)}) %reduce-scatter.2.cloned.1.call-update) | async-done | bytes 262160 | tf_op jit(solution)/shard_map/reduce_scatter | solution.py:66
  140.6 1.1 reshape.144
  141.8 3.1 %all-to-all-done.5 = bf16[8,56,640]{2,1,0:T(8,128)(2,1)S(1)} async-done(((bf16[8,56,640]{2,1,0:T(8,128)(2,1)}), bf16[8,56,640]{2,1,0:T(8,128)(2,1)S(1)}, u32[]{:S(2)}, u32[]{:S(2)}) %all-to-all-start.5) | async-done | bytes 573472 | tf_op jit(solution)/shard_map/all_to_all | solution.py:93
  145.3 17.1 %all_to_all.41 = bf16[4,120,640]{2,1,0:T(8,128)(2,1)S(1)} all-to-all(bf16[4,120,640]{2,1,0:T(8,128)(2,1)S(1)} %fusion.1), channel_id=1, replica_groups=mesh['z'=8,'yh'=4,'x'=4,'yl'=2,'core'=2] {'yh'}, dimensions={0} | all-to-all | bytes 1228800 | tf_op jit(solution)/shard_map/all_to_all | solution.py:103
  162.6 0.9 broadcast_in_dim.17
  163.4 11.6 %all-to-all-start.7 = ((bf16[8,56,640]{2,1,0:T(8,128)(2,1)}), bf16[8,56,640]{2,1,0:T(8,128)(2,1)S(1)}, u32[]{:S(2)}, u32[]{:S(2)}) async-start(bf16[8,56,640]{2,1,0:T(8,128)(2,1)} %broadcast_in_dim.17), calls=%async_computation.8 | async-start | bytes 1146880 | tf_op jit(solution)/shard_map/all_to_all | solution.py:32
  175.0 2.5 %convolution_convert_fusion.3 = bf16[512,448]{0,1:T(8,128)(2,1)} fusion(bf16[448,576]{1,0:T(8,128)(2,1)} %param.7, bf16[512,64]{1,0:T(8,128)(2,1)S(1)} %copy.27, bf16[512,512]{1,0:T(8,128)(2,1)} %bitcast.34), kind=kOutput, calls=%fused_computation.3 | convolution fusion | flops 265650176 | bytes 1564672 | tf_op jit(solution)/shard_map/dot_general | solution.py:15
  177.6 0.6 copy.32
  178.2 15.8 %all-to-all-done.7 = bf16[8,56,640]{2,1,0:T(8,128)(2,1)S(1)} async-done(((bf16[8,56,640]{2,1,0:T(8,128)(2,1)}), bf16[8,56,640]{2,1,0:T(8,128)(2,1)S(1)}, u32[]{:S(2)}, u32[]{:S(2)}) %all-to-all-start.7) | async-done | bytes 573472 | tf_op jit(solution)/shard_map/all_to_all | solution.py:32
  194.1 0.7 add.43
  194.8 0.8 copy.35
  (49 shorter events, 1.9 us)
Async XLA Ops:
  7.2 51.3 %copy-start = (bf16[512,2048]{1,0:T(8,128)(2,1)S(1)}, bf16[512,2048]{1,0:T(8,128)(2,1)}, u32[]{:S(2)}) copy-start(bf16[512,2048]{1,0:T(8,128)(2,1)} %param.10) | copy-start | bytes 6291460
  8.9 16.9 %all-to-all-start.1 = ((bf16[4,16,2048]{2,1,0:T(8,128)(2,1)}), bf16[4,16,2048]{2,1,0:T(8,128)(2,1)S(1)}, u32[]{:S(2)}, u32[]{:S(2)}) async-start(bf16[4,16,2048]{2,1,0:T(8,128)(2,1)} %broadcast_in_dim.12), calls=%async_computation.1 | async-start | bytes 524288 | tf_op jit(solution)/shard_map/all_to_all | solution.py:32
  25.8 5.4 %copy-start.1 = (bf16[4,16,2048]{2,1,0:T(8,128)(2,1)}, bf16[4,16,2048]{2,1,0:T(8,128)(2,1)S(1)}, u32[]{:S(2)}) copy-start(bf16[4,16,2048]{2,1,0:T(8,128)(2,1)S(1)} %all-to-all-done.1) | copy-start | bytes 786436
  25.8 19.2 %copy-start.5 = (f32[512]{0:T(512)S(1)}, f32[512]{0:T(512)}, u32[]{:S(2)}) copy-start(f32[512]{0:T(512)} %param.8) | copy-start | bytes 6148
  25.8 19.0 %all-to-all-start = ((f32[16,32,512]{2,1,0:T(8,128)}), f32[16,32,512]{2,1,0:T(8,128)S(1)}, u32[]{:S(2)}, u32[]{:S(2)}) async-start(f32[16,32,512]{2,1,0:T(8,128)} %bitcast.28), calls=%async_computation | async-start | bytes 2097152 | tf_op jit(solution)/shard_map/all_to_all | solution.py:26
  31.1 45.9 %all-gather.2.cloned.1.call-start = ((), (), s32[]{:S(2)}) async-start(), calls=%async_computation.9 | async-start | bytes 2359296 | tf_op jit(solution)/shard_map/all_gather | solution.py:56
  80.6 17.9 %all-to-all-start.3 = ((bf16[16,32,512]{2,1,0:T(8,128)(2,1)}), bf16[16,32,512]{2,1,0:T(8,128)(2,1)S(1)}, u32[]{:S(2)}, u32[]{:S(2)}) async-start(bf16[16,32,512]{2,1,0:T(8,128)(2,1)} %bitcast.4), calls=%async_computation.3 | async-start | bytes 1048576 | tf_op jit(solution)/shard_map/all_to_all | solution.py:26
  90.8 49.9 %reduce-scatter.2.cloned.1.call-start = ((), (), s32[]{:S(2)}) async-start(), calls=%async_computation.10 | async-start | bytes 2359296 | tf_op jit(solution)/shard_map/reduce_scatter | solution.py:66
  98.6 8.0 %copy-start.4 = (bf16[512,64]{0,1:T(8,128)(2,1)S(1)}, bf16[512,64]{0,1:T(8,128)(2,1)}, u32[]{:S(2)}) copy-start(bf16[512,64]{0,1:T(8,128)(2,1)} %param.11) | copy-start | bytes 196612
  99.8 17.3 %copy-start.3 = (bf16[512,448]{0,1:T(8,128)(2,1)S(1)}, bf16[512,448]{0,1:T(8,128)(2,1)}, u32[]{:S(2)}) copy-start(bf16[512,448]{0,1:T(8,128)(2,1)} %param.6) | copy-start | bytes 1376260
  99.8 16.3 %all-to-all-start.4 = ((bf16[16,40,512]{2,1,0:T(8,128)(2,1)}), bf16[16,40,512]{2,1,0:T(8,128)(2,1)S(1)}, u32[]{:S(2)}, u32[]{:S(2)}) async-start(bf16[16,40,512]{2,1,0:T(8,128)(2,1)} %broadcast_in_dim.15), calls=%async_computation.4 | async-start | bytes 1310720 | tf_op jit(solution)/shard_map/all_to_all | solution.py:32
  116.3 0.8 copy-start.2
  118.6 26.3 %all-to-all-start.5 = ((bf16[8,56,640]{2,1,0:T(8,128)(2,1)}), bf16[8,56,640]{2,1,0:T(8,128)(2,1)S(1)}, u32[]{:S(2)}, u32[]{:S(2)}) async-start(bf16[8,56,640]{2,1,0:T(8,128)(2,1)} %pad_maximum_fusion.1), calls=%async_computation.5 | async-start | bytes 1146880 | tf_op jit(solution)/shard_map/all_to_all | solution.py:93
  163.4 30.6 %all-to-all-start.7 = ((bf16[8,56,640]{2,1,0:T(8,128)(2,1)}), bf16[8,56,640]{2,1,0:T(8,128)(2,1)S(1)}, u32[]{:S(2)}, u32[]{:S(2)}) async-start(bf16[8,56,640]{2,1,0:T(8,128)(2,1)} %broadcast_in_dim.17), calls=%async_computation.8 | async-start | bytes 1146880 | tf_op jit(solution)/shard_map/all_to_all | solution.py:32
Sparse Core Ops, SparseCore 0:
  34.6 42.3 all-gather.1
  94.4 46.1 reduce-scatter.1

commit v2 on v1

--- a/solution.py
+++ b/solution.py
@@ -8,7 +8,6 @@
 DP = ("z", "yh")
 TENSOR = ("x", "yl", "core")
 GAIN_ROWS = 8
-LANES = 512
 
 
 def dot(a, b, dims):
@@ -32,27 +31,37 @@
     return lax.all_to_all(copies, axes, 0, 0, tiled=True)
 
 
+def shift(value, axis, parts, step):
+    return lax.ppermute(value, axis, [(i, (i + step) % parts) for i in range(parts)])
+
+
 def after(value, earlier):
     return lax.optimization_barrier((value, earlier))[0]
 
 
-def with_gain(down, gain):
+def pack(down, rope, gain):
     high, low = two_halves(gain)
     lanes = jnp.stack([high, low], axis=-2)
-    rows = [(0, 0)] * (lanes.ndim - 2) + [(0, down.shape[-2] - 2), (0, 0)]
-    return jnp.concatenate([down.astype(jnp.bfloat16), jnp.pad(lanes, rows)], axis=-1)
+    rows = [(0, 0)] * (lanes.ndim - 2) + [(0, rope.shape[-2] - 2), (0, 0)]
+    side = jnp.concatenate([rope.astype(jnp.bfloat16), jnp.pad(lanes, rows)], axis=-1)
+    return jnp.concatenate([down.astype(jnp.bfloat16), side], axis=-2)
 
 
-def parted(both, width):
-    lanes = both[..., :2, width:].astype(jnp.float32)
-    return both[..., :width], lanes[..., 0, :] + lanes[..., 1, :]
+def unpack(packed, near, share):
+    lanes = packed[..., near : near + 2, -share:].astype(jnp.float32)
+    gain = lanes[..., 0, :] + lanes[..., 1, :]
+    return packed[..., :near, :], packed[..., near:, :-share], gain
 
 
 def body(sizes, hidden, w_down, norm_gain, w_up, kv_grad, rope_grad):
     n_z, n_yh, n_t = sizes
     lat = norm_gain.shape[0]
-    width = w_down.shape[1]
-    w_up_near = spread(w_up, "yh", n_yh).reshape(-1, w_up.shape[1])
+    here = lax.axis_index("yh")
+    blocks = [shift(w_up, "yh", n_yh, k) for k in range(1, n_yh)]
+    circle = jnp.concatenate(blocks[::-1] + [w_up] + blocks[::-1], axis=0)
+    w_up_near = lax.dynamic_slice_in_dim(
+        circle, (n_yh - 1 - here) * w_up.shape[0], n_yh * w_up.shape[0], 0
+    )
     w_up_all = lax.all_gather(w_up_near, "z", axis=0, tiled=True)
 
     projected = scatter_sum(
@@ -83,33 +92,35 @@
         jnp.concatenate([proj_grad, high[None], low[None], fill], axis=0), TENSOR, n_t
     )
     rows = proj_grad.shape[0]
-    joint_grad = jnp.concatenate([joined[:, :rows].reshape(-1, lat), rope_grad], axis=1)
+    proj_all = joined[:, :rows].reshape(-1, lat)
+    joint_grad = jnp.concatenate([proj_all, rope_grad], axis=1)
     gain_group = jnp.sum(joined[:, rows : rows + 2].astype(jnp.float32), axis=(0, 1))
 
     hidden_grad = dot(joint_grad, w_down, ((1,), (1,))).astype(jnp.bfloat16)
 
-    down_part = dot(hidden, joint_grad, ((0,), (0,)))
-    packed = with_gain(down_part.reshape(n_z, -1, width), gain_group.reshape(n_z, -1))
+    down_part = dot(hidden, proj_all, ((0,), (0,))).reshape(n_z, -1, lat)
+    rope_part = dot(rope_grad, hidden, ((0,), (0,)))
+    near, share = down_part.shape[1], lat // n_z
+    packed = pack(
+        down_part,
+        rope_part.reshape(n_z, -1, rope_part.shape[1]),
+        gain_group.reshape(n_z, -1),
+    )
     arrived = lax.all_to_all(packed, "z", 0, 0, tiled=True).astype(jnp.float32)
-    down_sum, gain_sum = parted(jnp.sum(arrived, axis=0), width)
-    packed = with_gain(down_sum, gain_sum)
-    near = packed.shape[0]
-    up_rows = up_sum.shape[0] // n_yh
-    up_cut = up_sum.reshape(n_yh, up_rows, -1, LANES).transpose(0, 2, 1, 3)
-    up_cut = up_cut.reshape(n_yh, -1, LANES)
-    up_cut = jnp.pad(up_cut, [(0, 0), (0, 0), (0, packed.shape[1] - LANES)])
-    copies = jnp.broadcast_to(packed[None], (n_yh,) + packed.shape)
-    both = jnp.concatenate([copies, up_cut], axis=1)
-    arrived = lax.all_to_all(both, "yh", 0, 0, tiled=True)
-    up_grad = jnp.sum(arrived[:, near:, :LANES].astype(jnp.float32), axis=0)
-    up_grad = up_grad.reshape(-1, up_rows, LANES).transpose(1, 0, 2)
-    up_grad = up_grad.reshape(up_rows, -1).astype(jnp.bfloat16)
-    down_sum, gain_sum = parted(
-        jnp.sum(arrived[:, :near].astype(jnp.float32), axis=0), width
-    )
-    arrived = spread(with_gain(down_sum, gain_sum), "z", n_z)
-    down_grad, gain_grad = parted(arrived, width)
-    return (hidden_grad, down_grad.reshape(-1, width), gain_grad.reshape(-1), up_grad)
+    packed = pack(*unpack(jnp.sum(arrived, axis=0), near, share))
+    arrived = spread(after(packed, up_sum), "yh", n_yh).astype(jnp.float32)
+    total = jnp.sum(arrived, axis=0)
+    up_blocks = after(up_sum.reshape(n_yh, -1, up_sum.shape[1]), total)
+    up_grad = lax.dynamic_index_in_dim(up_blocks, here, 0, False).astype(jnp.float32)
+    for step in range(1, n_yh):
+        block = lax.dynamic_index_in_dim(up_blocks, lax.rem(here + step, n_yh), 0, False)
+        up_grad = up_grad + shift(block, "yh", n_yh, step).astype(jnp.float32)
+    up_grad = up_grad.astype(jnp.bfloat16)
+    arrived = spread(pack(*unpack(total, near, share)), "z", n_z)
+    down_grad, rope_down, gain_grad = unpack(arrived, near, share)
+    rope_down = rope_down.reshape(-1, rope_down.shape[-1]).T
+    down_grad = jnp.concatenate([down_grad.reshape(-1, lat), rope_down], axis=1)
+    return (hidden_grad, down_grad, gain_grad.reshape(-1), up_grad)
 
 
 def solution(mesh):

time: 203 us -> 195 us (0.961)
  the two profiles are of different devices: /device:TPU:23 before, /device:TPU:16 now
where the time goes in v2:
time: 195 us; the launch traced here: 194 us
  waiting for transfers between devices  68 us (35%)
  starting transfers between devices  52.9 us (27%)
  blocking collectives  39 us (20%)
  between operations  14.5 us (7%)
  matrix products  11.9 us (6%)
  local copies, waits for them, and re-layouts  4.86 us (2%)
  other arithmetic  2.85 us (1%)
    ppermute x6, starting transfers between devices, shift(): lax.ppermute(value, axis, [(i, (i + step) % parts) for i in range(parts)])  26.2 us
    all_to_all x2, waiting for transfers between devices, scatter_sum(): arrived = lax.all_to_all(pieces, axes, 0, 0, tiled=True)  25.7 us
    all_to_all x1, blocking collectives, body(): arrived = lax.all_to_all(packed, 'z', 0, 0, tiled=True).astype(jnp.float32)  25.5 us
    all_to_all x3, waiting for transfers between devices, spread(): return lax.all_to_all(copies, axes, 0, 0, tiled=True)  19.6 us
    all_to_all x3, starting transfers between devices, spread(): return lax.all_to_all(copies, axes, 0, 0, tiled=True)  17.6 us
    all_gather x1, waiting for transfers between devices, body(): w_up_all = lax.all_gather(w_up_near, 'z', axis=0, tiled=True)  17.4 us
    all_to_all x1, blocking collectives, spread(): return lax.all_to_all(copies, axes, 0, 0, tiled=True)  13.5 us
    dot_general x6, matrix products, dot(): lax.dot_general(a, b, (dims, ((), ())), preferred_element_type=jnp.float32)  11.9 us
  transfers between devices with their start and end apart: 13, of which 6 were waited for; matrix products, arithmetic and copies ran while one was open for 6% of the time, Pallas kernels for 0%

profile of v2, /device:TPU:16, one launch (start us, length us, event | category | flops | bytes accessed | tf_op | source)
XLA Modules:
  0.0 194.0 jit_solution(2886799170761103686)
XLA Ops:
  7.2 7.7 %collective-permute-start = (bf16[16,2048]{1,0:T(8,128)(2,1)}, bf16[16,2048]{1,0:T(8,128)(2,1)S(1)}, u32[]{:S(2)}, u32[]{:S(2)}) collective-permute-start(bf16[16,2048]{1,0:T(8,128)(2,1)} %param.9), channel_id=1, source_target_pairs={{0,48},{16,0},{32,16},{48,32},{1,49},{17,1},{33,17},{49,33},{2,50}... | collective-permute-start | bytes 196616 | tf_op jit(solution)/shard_map/ppermute | solution.py:35
  14.9 2.4 %collective-permute-start.1 = (bf16[16,2048]{1,0:T(8,128)(2,1)}, bf16[16,2048]{1,0:T(8,128)(2,1)S(1)}, u32[]{:S(2)}, u32[]{:S(2)}) collective-permute-start(bf16[16,2048]{1,0:T(8,128)(2,1)} %param.9), channel_id=1, source_target_pairs={{0,32},{16,48},{32,0},{48,16},{1,33},{17,49},{33,1},{49,17},{2,34}... | collective-permute-start | bytes 196616 | tf_op jit(solution)/shard_map/ppermute | solution.py:35
  17.3 5.0 %collective-permute-start.2 = (bf16[16,2048]{1,0:T(8,128)(2,1)}, bf16[16,2048]{1,0:T(8,128)(2,1)S(1)}, u32[]{:S(2)}, u32[]{:S(2)}) collective-permute-start(bf16[16,2048]{1,0:T(8,128)(2,1)} %param.9), channel_id=1, source_target_pairs={{0,16},{16,32},{32,48},{48,0},{1,17},{17,33},{33,49},{49,1},{2,18}... | collective-permute-start | bytes 196616 | tf_op jit(solution)/shard_map/ppermute | solution.py:35
  22.4 2.6 %fusion.4 = f32[512,512]{1,0:T(8,128)} fusion(bf16[512,448]{0,1:T(8,128)(2,1)} %param.6, bf16[448,576]{1,0:T(8,128)(2,1)} %param.7), kind=kOutput, calls=%fused_computation.14 | convolution fusion | flops 234881024 | bytes 1966080 | tf_op jit(solution)/shard_map/dot_general | solution.py:14
  25.0 3.8 %all-to-all-start = ((f32[16,32,512]{2,1,0:T(8,128)}), f32[16,32,512]{2,1,0:T(8,128)S(1)}, u32[]{:S(2)}, u32[]{:S(2)}) async-start(f32[16,32,512]{2,1,0:T(8,128)} %bitcast.37), calls=%async_computation | async-start | bytes 2097152 | tf_op jit(solution)/shard_map/all_to_all | solution.py:25
  29.0 0.7 constant_dynamic-slice_fusion
  29.7 15.6 %all-to-all-done = f32[16,32,512]{2,1,0:T(8,128)S(1)} async-done(((f32[16,32,512]{2,1,0:T(8,128)}), f32[16,32,512]{2,1,0:T(8,128)S(1)}, u32[]{:S(2)}, u32[]{:S(2)}) %all-to-all-start) | async-done | bytes 1048608 | tf_op jit(solution)/shard_map/all_to_all | solution.py:25
  45.7 13.5 %all_to_all.35 = bf16[16,32,512]{2,1,0:T(8,128)(2,1)S(1)} all-to-all(bf16[16,32,512]{2,1,0:T(8,128)(2,1)S(1)} %broadcast_in_dim.10), channel_id=1, replica_groups=mesh['z'=8,'yh'=4,'x'=4,'yl'=2,'core'=2] {'x','yl','core'}, dimensions={0} | all-to-all | bytes 1048576 | tf_op jit(solution)/shard_map/all_to_all | solution.py:31
  59.2 2.6 %convolution_convert_fusion = bf16[512,2048]{1,0:T(8,128)(2,1)} fusion(bf16[512,512]{1,0:T(8,128)(2,1)S(1)} %bitcast.43, bf16[512,2048]{1,0:T(8,128)(2,1)S(1)} %copy-done), kind=kOutput, calls=%fused_computation | convolution fusion | flops 1074790400 | bytes 4718592 | tf_op jit(solution)/shard_map/dot_general | solution.py:14
  61.8 17.4 %all-gather.2.cloned.1.call-done = bf16[512,2048]{1,0:T(8,128)(2,1)} async-done(((bf16[64,2048]{1,0:T(8,128)(2,1)}), bf16[512,2048]{1,0:T(8,128)(2,1)}) %all-gather.2.cloned.1.call-update) | async-done | bytes 2097168 | tf_op jit(solution)/shard_map/all_gather | solution.py:65
  79.2 3.7 %convolution_convert_fusion.1 = bf16[512,512]{0,1:T(8,128)(2,1)} fusion(bf16[512,2048]{1,0:T(8,128)(2,1)} %all-gather.2.cloned.1.call-done, bf16[512,2048]{1,0:T(8,128)(2,1)S(1)} %copy-done), kind=kOutput, calls=%fused_computation.1 | convolution fusion | flops 1074003968 | bytes 4718592 | tf_op jit(solution)/shard_map/dot_general | solution.py:14
  82.9 5.3 %all-to-all-start.2 = ((bf16[16,32,512]{2,1,0:T(8,128)(2,1)}), bf16[16,32,512]{2,1,0:T(8,128)(2,1)S(1)}, u32[]{:S(2)}, u32[]{:S(2)}) async-start(bf16[16,32,512]{2,1,0:T(8,128)(2,1)} %bitcast.42), calls=%async_computation.2 | async-start | bytes 1048576 | tf_op jit(solution)/shard_map/all_to_all | solution.py:25
  88.3 0.6 reduce-scatter.2.cloned.1.call-update
  88.9 10.1 %all-to-all-done.2 = bf16[16,32,512]{2,1,0:T(8,128)(2,1)S(1)} async-done(((bf16[16,32,512]{2,1,0:T(8,128)(2,1)}), bf16[16,32,512]{2,1,0:T(8,128)(2,1)S(1)}, u32[]{:S(2)}, u32[]{:S(2)}) %all-to-all-start.2) | async-done | bytes 524320 | tf_op jit(solution)/shard_map/all_to_all | solution.py:25
  99.4 0.9 broadcast_in_dim.12
  100.3 3.6 %all-to-all-start.3 = ((bf16[16,40,512]{2,1,0:T(8,128)(2,1)}), bf16[16,40,512]{2,1,0:T(8,128)(2,1)S(1)}, u32[]{:S(2)}, u32[]{:S(2)}) async-start(bf16[16,40,512]{2,1,0:T(8,128)(2,1)} %broadcast_in_dim.12), calls=%async_computation.3 | async-start | bytes 1310720 | tf_op jit(solution)/shard_map/all_to_all | solution.py:31
  104.2 12.0 %all-to-all-done.3 = bf16[16,40,512]{2,1,0:T(8,128)(2,1)S(1)} async-done(((bf16[16,40,512]{2,1,0:T(8,128)(2,1)}), bf16[16,40,512]{2,1,0:T(8,128)(2,1)S(1)}, u32[]{:S(2)}, u32[]{:S(2)}) %all-to-all-start.3) | async-done | bytes 655392 | tf_op jit(solution)/shard_map/all_to_all | solution.py:31
  116.4 0.4 convolution_convert_fusion.2
  117.2 25.5 %all_to_all.36 = bf16[8,64,512]{2,1,0:T(8,128)(2,1)S(1)} all-to-all(bf16[8,64,512]{2,1,0:T(8,128)(2,1)S(1)} %maximum_maximum_fusion), channel_id=1, replica_groups=mesh['z'=8,'yh'=4,'x'=4,'yl'=2,'core'=2] {'z'}, dimensions={0} | all-to-all | bytes 1048576 | tf_op jit(solution)/shard_map/all_to_all | solution.py:109
  143.1 0.7 broadcast_in_dim.13
  143.8 8.3 %all-to-all-start.5 = ((bf16[4,64,512]{2,1,0:T(8,128)(2,1)}), bf16[4,64,512]{2,1,0:T(8,128)(2,1)S(1)}, u32[]{:S(2)}, u32[]{:S(2)}) async-start(bf16[4,64,512]{2,1,0:T(8,128)(2,1)} %broadcast_in_dim.13), calls=%async_computation.6 | async-start | bytes 524288 | tf_op jit(solution)/shard_map/all_to_all | solution.py:31
  152.3 7.6 %all-to-all-done.5 = bf16[4,64,512]{2,1,0:T(8,128)(2,1)S(1)} async-done(((bf16[4,64,512]{2,1,0:T(8,128)(2,1)}), bf16[4,64,512]{2,1,0:T(8,128)(2,1)S(1)}, u32[]{:S(2)}, u32[]{:S(2)}) %all-to-all-start.5) | async-done | bytes 262176 | tf_op jit(solution)/shard_map/all_to_all | solution.py:31
  160.1 0.8 broadcast_in_dim.14
  160.9 5.7 %all-to-all-start.6 = ((bf16[8,64,512]{2,1,0:T(8,128)(2,1)}), bf16[8,64,512]{2,1,0:T(8,128)(2,1)S(1)}, u32[]{:S(2)}, u32[]{:S(2)}) async-start(bf16[8,64,512]{2,1,0:T(8,128)(2,1)} %broadcast_in_dim.14), calls=%async_computation.7 | async-start | bytes 1048576 | tf_op jit(solution)/shard_map/all_to_all | solution.py:31
  166.7 1.9 collective-permute-start.3
  168.6 7.1 %collective-permute-start.4 = (bf16[16,2048]{1,0:T(8,128)(2,1)S(1)}, bf16[16,2048]{1,0:T(8,128)(2,1)S(1)}, u32[]{:S(2)}, u32[]{:S(2)}) collective-permute-start(bf16[16,2048]{1,0:T(8,128)(2,1)S(1)} %get-tuple-element.14), channel_id=1, source_target_pairs={{0,32},{16,48},{32,0},{48,16},{1,33},{17,49},{33,1},{49,17},{2,34}... | collective-permute-start | bytes 196616 | tf_op jit(solution)/shard_map/ppermute | solution.py:35
  175.7 2.0 %collective-permute-start.5 = (bf16[16,2048]{1,0:T(8,128)(2,1)S(1)}, bf16[16,2048]{1,0:T(8,128)(2,1)S(1)}, u32[]{:S(2)}, u32[]{:S(2)}) collective-permute-start(bf16[16,2048]{1,0:T(8,128)(2,1)S(1)} %get-tuple-element.13), channel_id=1, source_target_pairs={{0,48},{16,0},{32,16},{48,32},{1,49},{17,1},{33,17},{49,33},{2,50}... | collective-permute-start | bytes 196616 | tf_op jit(solution)/shard_map/ppermute | solution.py:35
  177.7 2.4 %convolution_convert_fusion.3 = bf16[512,448]{0,1:T(8,128)(2,1)} fusion(bf16[448,576]{1,0:T(8,128)(2,1)} %param.7, bf16[512,64]{1,0:T(8,128)(2,1)S(1)} %copy.22, bf16[512,512]{1,0:T(8,128)(2,1)S(1)} %bitcast.39), kind=kOutput, calls=%fused_computation.3 | convolution fusion | flops 265650176 | bytes 1564672 | tf_op jit(solution)/shard_map/dot_general | solution.py:14
  180.1 4.6 %collective-permute-done.5 = bf16[16,2048]{1,0:T(8,128)(2,1)S(1)} collective-permute-done((bf16[16,2048]{1,0:T(8,128)(2,1)S(1)}, bf16[16,2048]{1,0:T(8,128)(2,1)S(1)}, u32[]{:S(2)}, u32[]{:S(2)}) %collective-permute-start.5) | collective-permute-done | bytes 65568 | tf_op jit(solution)/shard_map/ppermute | solution.py:35
  184.7 0.7 fusion.8
  185.6 0.7 add.76
  186.3 0.9 pad_maximum_fusion
  (75 shorter events, 2.7 us)
Async XLA Ops:
  7.2 52.0 %copy-start = (bf16[512,2048]{1,0:T(8,128)(2,1)S(1)}, bf16[512,2048]{1,0:T(8,128)(2,1)}, u32[]{:S(2)}) copy-start(bf16[512,2048]{1,0:T(8,128)(2,1)} %param.10) | copy-start | bytes 6291460
  7.2 21.7 %copy-start.6 = (bf16[16,2048]{1,0:T(8,128)(2,1)S(1)}, bf16[16,2048]{1,0:T(8,128)(2,1)}, u32[]{:S(2)}) copy-start(bf16[16,2048]{1,0:T(8,128)(2,1)} %param.9) | copy-start | bytes 196612
  7.2 21.6 %collective-permute-start = (bf16[16,2048]{1,0:T(8,128)(2,1)}, bf16[16,2048]{1,0:T(8,128)(2,1)S(1)}, u32[]{:S(2)}, u32[]{:S(2)}) collective-permute-start(bf16[16,2048]{1,0:T(8,128)(2,1)} %param.9), channel_id=1, source_target_pairs={{0,48},{16,0},{32,16},{48,32},{1,49},{17,1},{33,17},{49,33},{2,50}... | collective-permute-start | bytes 196616 | tf_op jit(solution)/shard_map/ppermute | solution.py:35
  14.9 13.9 %collective-permute-start.1 = (bf16[16,2048]{1,0:T(8,128)(2,1)}, bf16[16,2048]{1,0:T(8,128)(2,1)S(1)}, u32[]{:S(2)}, u32[]{:S(2)}) collective-permute-start(bf16[16,2048]{1,0:T(8,128)(2,1)} %param.9), channel_id=1, source_target_pairs={{0,32},{16,48},{32,0},{48,16},{1,33},{17,49},{33,1},{49,17},{2,34}... | collective-permute-start | bytes 196616 | tf_op jit(solution)/shard_map/ppermute | solution.py:35
  17.3 11.6 %collective-permute-start.2 = (bf16[16,2048]{1,0:T(8,128)(2,1)}, bf16[16,2048]{1,0:T(8,128)(2,1)S(1)}, u32[]{:S(2)}, u32[]{:S(2)}) collective-permute-start(bf16[16,2048]{1,0:T(8,128)(2,1)} %param.9), channel_id=1, source_target_pairs={{0,16},{16,32},{32,48},{48,0},{1,17},{17,33},{33,49},{49,1},{2,18}... | collective-permute-start | bytes 196616 | tf_op jit(solution)/shard_map/ppermute | solution.py:35
  25.0 20.6 %copy-start.7 = (f32[512]{0:T(512)S(1)}, f32[512]{0:T(512)}, u32[]{:S(2)}) copy-start(f32[512]{0:T(512)} %param.8) | copy-start | bytes 6148
  25.0 20.4 %all-to-all-start = ((f32[16,32,512]{2,1,0:T(8,128)}), f32[16,32,512]{2,1,0:T(8,128)S(1)}, u32[]{:S(2)}, u32[]{:S(2)}) async-start(f32[16,32,512]{2,1,0:T(8,128)} %bitcast.37), calls=%async_computation | async-start | bytes 2097152 | tf_op jit(solution)/shard_map/all_to_all | solution.py:25
  28.8 50.5 %all-gather.2.cloned.1.call-start = ((), (), s32[]{:S(2)}) async-start(), calls=%async_computation.8 | async-start | bytes 2359296 | tf_op jit(solution)/shard_map/all_gather | solution.py:65
  82.9 16.2 %all-to-all-start.2 = ((bf16[16,32,512]{2,1,0:T(8,128)(2,1)}), bf16[16,32,512]{2,1,0:T(8,128)(2,1)S(1)}, u32[]{:S(2)}, u32[]{:S(2)}) async-start(bf16[16,32,512]{2,1,0:T(8,128)(2,1)} %bitcast.42), calls=%async_computation.2 | async-start | bytes 1048576 | tf_op jit(solution)/shard_map/all_to_all | solution.py:25
  88.2 54.9 %reduce-scatter.2.cloned.1.call-start = ((), (), s32[]{:S(2)}) async-start(), calls=%async_computation.9 | async-start | bytes 2359296 | tf_op jit(solution)/shard_map/reduce_scatter | solution.py:75
  88.3 15.6 %copy-start.1 = (bf16[512,448]{0,1:T(8,128)(2,1)S(1)}, bf16[512,448]{0,1:T(8,128)(2,1)}, u32[]{:S(2)}) copy-start(bf16[512,448]{0,1:T(8,128)(2,1)} %param.6) | copy-start | bytes 1376260
  88.3 15.6 %copy-start.4 = (bf16[512,64]{0,1:T(8,128)(2,1)S(1)}, bf16[512,64]{0,1:T(8,128)(2,1)}, u32[]{:S(2)}) copy-start(bf16[512,64]{0,1:T(8,128)(2,1)} %param.11) | copy-start | bytes 196612
  100.3 15.9 %all-to-all-start.3 = ((bf16[16,40,512]{2,1,0:T(8,128)(2,1)}), bf16[16,40,512]{2,1,0:T(8,128)(2,1)S(1)}, u32[]{:S(2)}, u32[]{:S(2)}) async-start(bf16[16,40,512]{2,1,0:T(8,128)(2,1)} %broadcast_in_dim.12), calls=%async_computation.3 | async-start | bytes 1310720 | tf_op jit(solution)/shard_map/all_to_all | solution.py:31
  116.4 0.8 copy-start.2
  142.9 34.8 %copy-start.3 = (bf16[16,32,512]{2,1,0:T(8,128)(2,1)S(1)}, bf16[16,32,512]{2,1,0:T(8,128)(2,1)}, u32[]{:S(2)}) copy-start(bf16[16,32,512]{2,1,0:T(8,128)(2,1)} %copy-done.2) | copy-start | bytes 1572868
  143.8 16.0 %all-to-all-start.5 = ((bf16[4,64,512]{2,1,0:T(8,128)(2,1)}), bf16[4,64,512]{2,1,0:T(8,128)(2,1)S(1)}, u32[]{:S(2)}, u32[]{:S(2)}) async-start(bf16[4,64,512]{2,1,0:T(8,128)(2,1)} %broadcast_in_dim.13), calls=%async_computation.6 | async-start | bytes 524288 | tf_op jit(solution)/shard_map/all_to_all | solution.py:31
  152.2 14.4 %copy-start.5 = (bf16[64,2048]{1,0:T(8,128)(2,1)S(1)}, bf16[64,2048]{1,0:T(8,128)(2,1)}, u32[]{:S(2)}) copy-start(bf16[64,2048]{1,0:T(8,128)(2,1)} %reduce-scatter.2.cloned.1.call-done) | copy-start | bytes 786436
  160.9 24.5 %all-to-all-start.6 = ((bf16[8,64,512]{2,1,0:T(8,128)(2,1)}), bf16[8,64,512]{2,1,0:T(8,128)(2,1)S(1)}, u32[]{:S(2)}, u32[]{:S(2)}) async-start(bf16[8,64,512]{2,1,0:T(8,128)(2,1)} %broadcast_in_dim.14), calls=%async_computation.7 | async-start | bytes 1048576 | tf_op jit(solution)/shard_map/all_to_all | solution.py:31
  166.7 13.4 %collective-permute-start.3 = (bf16[16,2048]{1,0:T(8,128)(2,1)S(1)}, bf16[16,2048]{1,0:T(8,128)(2,1)S(1)}, u32[]{:S(2)}, u32[]{:S(2)}) collective-permute-start(bf16[16,2048]{1,0:T(8,128)(2,1)S(1)} %get-tuple-element.12), channel_id=1, source_target_pairs={{0,16},{16,32},{32,48},{48,0},{1,17},{17,33},{33,49},{49,1},{2,18}... | collective-permute-start | bytes 196616 | tf_op jit(solution)/shard_map/ppermute | solution.py:35
  168.6 11.5 %collective-permute-start.4 = (bf16[16,2048]{1,0:T(8,128)(2,1)S(1)}, bf16[16,2048]{1,0:T(8,128)(2,1)S(1)}, u32[]{:S(2)}, u32[]{:S(2)}) collective-permute-start(bf16[16,2048]{1,0:T(8,128)(2,1)S(1)} %get-tuple-element.14), channel_id=1, source_target_pairs={{0,32},{16,48},{32,0},{48,16},{1,33},{17,49},{33,1},{49,17},{2,34}... | collective-permute-start | bytes 196616 | tf_op jit(solution)/shard_map/ppermute | solution.py:35
  175.7 9.0 %collective-permute-start.5 = (bf16[16,2048]{1,0:T(8,128)(2,1)S(1)}, bf16[16,2048]{1,0:T(8,128)(2,1)S(1)}, u32[]{:S(2)}, u32[]{:S(2)}) collective-permute-start(bf16[16,2048]{1,0:T(8,128)(2,1)S(1)} %get-tuple-element.13), channel_id=1, source_target_pairs={{0,48},{16,0},{32,16},{48,32},{1,49},{17,1},{33,17},{49,33},{2,50}... | collective-permute-start | bytes 196616 | tf_op jit(solution)/shard_map/ppermute | solution.py:35
Sparse Core Ops, SparseCore 0:
  32.2 46.9 all-gather.1
  91.9 50.4 reduce-scatter.1

commit v3 on v2

--- a/solution.py
+++ b/solution.py
@@ -73,7 +73,7 @@
 
     up_part = dot(latent_all, kv_grad, ((0,), (0,))).astype(jnp.bfloat16)
     up_sum = lax.psum_scatter(up_part, "z", scatter_dimension=0, tiled=True)
-    grad_part = dot(kv_grad, after(w_up_all, up_part), ((1,), (1,)))
+    grad_part = dot(kv_grad, after(w_up_all, latent_all), ((1,), (1,)))
     latent_grad = scatter_sum(grad_part.astype(jnp.bfloat16), TENSOR, n_t)
     gain_share = jnp.sum(latent_grad * projected * inv_rms, axis=0)
     scaled = norm_gain * latent_grad
@@ -107,7 +107,8 @@
         gain_group.reshape(n_z, -1),
     )
     arrived = lax.all_to_all(packed, "z", 0, 0, tiled=True).astype(jnp.float32)
-    packed = pack(*unpack(jnp.sum(arrived, axis=0), near, share))
+    near_sum = after(jnp.sum(arrived, axis=0), hidden_grad)
+    packed = pack(*unpack(near_sum, near, share))
     arrived = spread(after(packed, up_sum), "yh", n_yh).astype(jnp.float32)
     total = jnp.sum(arrived, axis=0)
     up_blocks = after(up_sum.reshape(n_yh, -1, up_sum.shape[1]), total)

time: 195 us -> 191 us (0.979)
  the two profiles are of different devices: /device:TPU:16 before, /device:TPU:4 now
where the time goes in v3:
time: 191 us; the launch traced here: 190 us
  waiting for transfers between devices  57.2 us (30%)
  blocking collectives  51.5 us (27%)
  starting transfers between devices  46.2 us (24%)
  between operations  14.4 us (8%)
  matrix products  12 us (6%)
  local copies, waits for them, and re-layouts  4.98 us (3%)
  other arithmetic  3.65 us (2%)
    all_to_all x2, blocking collectives, spread(): return lax.all_to_all(copies, axes, 0, 0, tiled=True)  31.4 us
    ppermute x6, starting transfers between devices, shift(): lax.ppermute(value, axis, [(i, (i + step) % parts) for i in range(parts)])  25.2 us
    all_to_all x1, waiting for transfers between devices, body(): arrived = lax.all_to_all(packed, 'z', 0, 0, tiled=True).astype(jnp.float32)  20.5 us
    all_to_all x1, blocking collectives, scatter_sum(): arrived = lax.all_to_all(pieces, axes, 0, 0, tiled=True)  20.2 us
    dot_general x6, matrix products, dot(): lax.dot_general(a, b, (dims, ((), ())), preferred_element_type=jnp.float32)  12 us
    all_gather x1, waiting for transfers between devices, body(): w_up_all = lax.all_gather(w_up_near, 'z', axis=0, tiled=True)  11.5 us
    ppermute x6, waiting for transfers between devices, shift(): lax.ppermute(value, axis, [(i, (i + step) % parts) for i in range(parts)])  11.1 us
    all_to_all x2, starting transfers between devices, spread(): return lax.all_to_all(copies, axes, 0, 0, tiled=True)  11 us
  transfers between devices with their start and end apart: 12, of which 9 were waited for; matrix products, arithmetic and copies ran while one was open for 6% of the time, Pallas kernels for 0%

profile of v3, /device:TPU:4, one launch (start us, length us, event | category | flops | bytes accessed | tf_op | source)
XLA Modules:
  0.0 189.9 jit_solution(10993642234592583667)
XLA Ops:
  7.2 6.3 %collective-permute-start = (bf16[16,2048]{1,0:T(8,128)(2,1)}, bf16[16,2048]{1,0:T(8,128)(2,1)S(1)}, u32[]{:S(2)}, u32[]{:S(2)}) collective-permute-start(bf16[16,2048]{1,0:T(8,128)(2,1)} %param.9), channel_id=1, source_target_pairs={{0,48},{16,0},{32,16},{48,32},{1,49},{17,1},{33,17},{49,33},{2,50}... | collective-permute-start | bytes 196616 | tf_op jit(solution)/shard_map/ppermute | solution.py:35
  13.5 3.8 %collective-permute-start.1 = (bf16[16,2048]{1,0:T(8,128)(2,1)}, bf16[16,2048]{1,0:T(8,128)(2,1)S(1)}, u32[]{:S(2)}, u32[]{:S(2)}) collective-permute-start(bf16[16,2048]{1,0:T(8,128)(2,1)} %param.9), channel_id=1, source_target_pairs={{0,32},{16,48},{32,0},{48,16},{1,33},{17,49},{33,1},{49,17},{2,34}... | collective-permute-start | bytes 196616 | tf_op jit(solution)/shard_map/ppermute | solution.py:35
  17.4 4.5 %collective-permute-start.2 = (bf16[16,2048]{1,0:T(8,128)(2,1)}, bf16[16,2048]{1,0:T(8,128)(2,1)S(1)}, u32[]{:S(2)}, u32[]{:S(2)}) collective-permute-start(bf16[16,2048]{1,0:T(8,128)(2,1)} %param.9), channel_id=1, source_target_pairs={{0,16},{16,32},{32,48},{48,0},{1,17},{17,33},{33,49},{49,1},{2,18}... | collective-permute-start | bytes 196616 | tf_op jit(solution)/shard_map/ppermute | solution.py:35
  21.9 3.6 %collective-permute-done.1 = bf16[16,2048]{1,0:T(8,128)(2,1)S(1)} collective-permute-done((bf16[16,2048]{1,0:T(8,128)(2,1)}, bf16[16,2048]{1,0:T(8,128)(2,1)S(1)}, u32[]{:S(2)}, u32[]{:S(2)}) %collective-permute-start.1) | collective-permute-done | bytes 65568 | tf_op jit(solution)/shard_map/ppermute | solution.py:35
  26.0 0.8 constant_dynamic-update-slice_fusion.3
  26.9 0.7 constant_dynamic-slice_fusion
  27.6 1.6 fusion.4
  29.3 20.2 %all_to_all.35 = f32[16,32,512]{2,1,0:T(8,128)S(1)} all-to-all(f32[16,32,512]{2,1,0:T(8,128)S(1)} %bitcast.37), channel_id=1, replica_groups=mesh['z'=8,'yh'=4,'x'=4,'yl'=2,'core'=2] {'x','yl','core'}, dimensions={0} | all-to-all | bytes 2097152 | tf_op jit(solution)/shard_map/all_to_all | solution.py:25
  49.8 14.1 %all_to_all.36 = bf16[16,32,512]{2,1,0:T(8,128)(2,1)} all-to-all(bf16[16,32,512]{2,1,0:T(8,128)(2,1)S(1)} %broadcast_in_dim.10), channel_id=1, replica_groups=mesh['z'=8,'yh'=4,'x'=4,'yl'=2,'core'=2] {'x','yl','core'}, dimensions={0} | all-to-all | bytes 1048576 | tf_op jit(solution)/shard_map/all_to_all | solution.py:31
  63.9 11.5 %all-gather.2.cloned.1.call-done = bf16[512,2048]{1,0:T(8,128)(2,1)} async-done(((bf16[64,2048]{1,0:T(8,128)(2,1)}), bf16[512,2048]{1,0:T(8,128)(2,1)}) %all-gather.2.cloned.1.call-update) | async-done | bytes 2097168 | tf_op jit(solution)/shard_map/all_gather | solution.py:65
  75.4 3.7 %convolution_convert_fusion.1 = bf16[512,512]{0,1:T(8,128)(2,1)} fusion(bf16[512,2048]{1,0:T(8,128)(2,1)} %all-gather.2.cloned.1.call-done, bf16[512,2048]{1,0:T(8,128)(2,1)S(1)} %copy-done), kind=kOutput, calls=%fused_computation.1 | convolution fusion | flops 1074003968 | bytes 4718592 | tf_op jit(solution)/shard_map/dot_general | solution.py:14
  79.0 5.7 %all-to-all-start.2 = ((bf16[16,32,512]{2,1,0:T(8,128)(2,1)}), bf16[16,32,512]{2,1,0:T(8,128)(2,1)S(1)}, u32[]{:S(2)}, u32[]{:S(2)}) async-start(bf16[16,32,512]{2,1,0:T(8,128)(2,1)} %bitcast.42), calls=%async_computation.2 | async-start | bytes 1048576 | tf_op jit(solution)/shard_map/all_to_all | solution.py:25
  84.9 3.7 %convolution_convert_fusion = bf16[512,2048]{1,0:T(8,128)(2,1)} fusion(bf16[512,512]{1,0:T(8,128)(2,1)} %bitcast.43, bf16[512,2048]{1,0:T(8,128)(2,1)S(1)} %copy-done), kind=kOutput, calls=%fused_computation | convolution fusion | flops 1074790400 | bytes 4718592 | tf_op jit(solution)/shard_map/dot_general | solution.py:14
  88.6 4.5 %all-to-all-done.2 = bf16[16,32,512]{2,1,0:T(8,128)(2,1)S(1)} async-done(((bf16[16,32,512]{2,1,0:T(8,128)(2,1)}), bf16[16,32,512]{2,1,0:T(8,128)(2,1)S(1)}, u32[]{:S(2)}, u32[]{:S(2)}) %all-to-all-start.2) | async-done | bytes 524320 | tf_op jit(solution)/shard_map/all_to_all | solution.py:25
  93.5 0.9 broadcast_in_dim.12
  94.4 6.1 %all-to-all-start.3 = ((bf16[16,40,512]{2,1,0:T(8,128)(2,1)}), bf16[16,40,512]{2,1,0:T(8,128)(2,1)S(1)}, u32[]{:S(2)}, u32[]{:S(2)}) async-start(bf16[16,40,512]{2,1,0:T(8,128)(2,1)} %broadcast_in_dim.12), calls=%async_computation.3 | async-start | bytes 1310720 | tf_op jit(solution)/shard_map/all_to_all | solution.py:31
  100.7 9.4 %all-to-all-done.3 = bf16[16,40,512]{2,1,0:T(8,128)(2,1)S(1)} async-done(((bf16[16,40,512]{2,1,0:T(8,128)(2,1)}), bf16[16,40,512]{2,1,0:T(8,128)(2,1)S(1)}, u32[]{:S(2)}, u32[]{:S(2)}) %all-to-all-start.3) | async-done | bytes 655392 | tf_op jit(solution)/shard_map/all_to_all | solution.py:31
  111.2 0.9 maximum_maximum_fusion
  112.0 4.1 %all-to-all-start.4 = ((bf16[8,64,512]{2,1,0:T(8,128)(2,1)}), bf16[8,64,512]{2,1,0:T(8,128)(2,1)S(1)}, u32[]{:S(2)}, u32[]{:S(2)}) async-start(bf16[8,64,512]{2,1,0:T(8,128)(2,1)} %maximum_maximum_fusion), calls=%async_computation.4 | async-start | bytes 1048576 | tf_op jit(solution)/shard_map/all_to_all | solution.py:109
  116.3 2.4 %convolution_convert_fusion.3 = bf16[512,448]{0,1:T(8,128)(2,1)} fusion(bf16[448,576]{1,0:T(8,128)(2,1)} %param.7, bf16[512,64]{1,0:T(8,128)(2,1)S(1)} %copy.22, bf16[512,512]{1,0:T(8,128)(2,1)S(1)} %bitcast.39), kind=kOutput, calls=%fused_computation.3 | convolution fusion | flops 265650176 | bytes 1564672 | tf_op jit(solution)/shard_map/dot_general | solution.py:14
  118.7 20.5 %all-to-all-done.4 = bf16[8,64,512]{2,1,0:T(8,128)(2,1)S(1)} async-done(((bf16[8,64,512]{2,1,0:T(8,128)(2,1)}), bf16[8,64,512]{2,1,0:T(8,128)(2,1)S(1)}, u32[]{:S(2)}, u32[]{:S(2)}) %all-to-all-start.4) | async-done | bytes 524320 | tf_op jit(solution)/shard_map/all_to_all | solution.py:109
  139.7 17.3 %all_to_all.37 = bf16[4,64,512]{2,1,0:T(8,128)(2,1)S(1)} all-to-all(bf16[4,64,512]{2,1,0:T(8,128)(2,1)S(1)} %broadcast_in_dim.13), channel_id=1, replica_groups=mesh['z'=8,'yh'=4,'x'=4,'yl'=2,'core'=2] {'yh'}, dimensions={0} | all-to-all | bytes 524288 | tf_op jit(solution)/shard_map/all_to_all | solution.py:31
  157.2 0.8 broadcast_in_dim.14
  158.0 4.9 %all-to-all-start.6 = ((bf16[8,64,512]{2,1,0:T(8,128)(2,1)}), bf16[8,64,512]{2,1,0:T(8,128)(2,1)S(1)}, u32[]{:S(2)}, u32[]{:S(2)}) async-start(bf16[8,64,512]{2,1,0:T(8,128)(2,1)} %broadcast_in_dim.14), calls=%async_computation.7 | async-start | bytes 1048576 | tf_op jit(solution)/shard_map/all_to_all | solution.py:31
  162.9 2.9 %collective-permute-start.5 = (bf16[16,2048]{1,0:T(8,128)(2,1)S(1)}, bf16[16,2048]{1,0:T(8,128)(2,1)S(1)}, u32[]{:S(2)}, u32[]{:S(2)}) collective-permute-start(bf16[16,2048]{1,0:T(8,128)(2,1)S(1)} %get-tuple-element.15), channel_id=1, source_target_pairs={{0,48},{16,0},{32,16},{48,32},{1,49},{17,1},{33,17},{49,33},{2,50}... | collective-permute-start | bytes 196616 | tf_op jit(solution)/shard_map/ppermute | solution.py:35
  165.8 5.8 %collective-permute-start.4 = (bf16[16,2048]{1,0:T(8,128)(2,1)S(1)}, bf16[16,2048]{1,0:T(8,128)(2,1)S(1)}, u32[]{:S(2)}, u32[]{:S(2)}) collective-permute-start(bf16[16,2048]{1,0:T(8,128)(2,1)S(1)} %get-tuple-element.16), channel_id=1, source_target_pairs={{0,32},{16,48},{32,0},{48,16},{1,33},{17,49},{33,1},{49,17},{2,34}... | collective-permute-start | bytes 196616 | tf_op jit(solution)/shard_map/ppermute | solution.py:35
  171.7 1.9 %collective-permute-start.3 = (bf16[16,2048]{1,0:T(8,128)(2,1)S(1)}, bf16[16,2048]{1,0:T(8,128)(2,1)S(1)}, u32[]{:S(2)}, u32[]{:S(2)}) collective-permute-start(bf16[16,2048]{1,0:T(8,128)(2,1)S(1)} %get-tuple-element.14), channel_id=1, source_target_pairs={{0,16},{16,32},{32,48},{48,0},{1,17},{17,33},{33,49},{49,1},{2,18}... | collective-permute-start | bytes 196616 | tf_op jit(solution)/shard_map/ppermute | solution.py:35
  173.6 2.5 %collective-permute-done.4 = bf16[16,2048]{1,0:T(8,128)(2,1)S(1)} collective-permute-done((bf16[16,2048]{1,0:T(8,128)(2,1)S(1)}, bf16[16,2048]{1,0:T(8,128)(2,1)S(1)}, u32[]{:S(2)}, u32[]{:S(2)}) %collective-permute-start.4) | collective-permute-done | bytes 65568 | tf_op jit(solution)/shard_map/ppermute | solution.py:35
  176.1 4.6 %collective-permute-done.3 = bf16[16,2048]{1,0:T(8,128)(2,1)S(1)} collective-permute-done((bf16[16,2048]{1,0:T(8,128)(2,1)S(1)}, bf16[16,2048]{1,0:T(8,128)(2,1)S(1)}, u32[]{:S(2)}, u32[]{:S(2)}) %collective-permute-start.3) | collective-permute-done | bytes 65568 | tf_op jit(solution)/shard_map/ppermute | solution.py:35
  180.6 0.7 fusion.8
  181.5 0.7 add.76
  182.2 0.9 pad_maximum_fusion
  (72 shorter events, 3.7 us)
Async XLA Ops:
  7.2 68.2 %copy-start = (bf16[512,2048]{1,0:T(8,128)(2,1)S(1)}, bf16[512,2048]{1,0:T(8,128)(2,1)}, u32[]{:S(2)}) copy-start(bf16[512,2048]{1,0:T(8,128)(2,1)} %param.10) | copy-start | bytes 6291460
  7.2 68.2 %all-gather.2.cloned.1.call-start = ((), (), s32[]{:S(2)}) async-start(), calls=%async_computation.8 | async-start | bytes 2359296 | tf_op jit(solution)/shard_map/all_gather | solution.py:65
  7.2 14.6 %collective-permute-start = (bf16[16,2048]{1,0:T(8,128)(2,1)}, bf16[16,2048]{1,0:T(8,128)(2,1)S(1)}, u32[]{:S(2)}, u32[]{:S(2)}) collective-permute-start(bf16[16,2048]{1,0:T(8,128)(2,1)} %param.9), channel_id=1, source_target_pairs={{0,48},{16,0},{32,16},{48,32},{1,49},{17,1},{33,17},{49,33},{2,50}... | collective-permute-start | bytes 196616 | tf_op jit(solution)/shard_map/ppermute | solution.py:35
  13.5 12.0 %collective-permute-start.1 = (bf16[16,2048]{1,0:T(8,128)(2,1)}, bf16[16,2048]{1,0:T(8,128)(2,1)S(1)}, u32[]{:S(2)}, u32[]{:S(2)}) collective-permute-start(bf16[16,2048]{1,0:T(8,128)(2,1)} %param.9), channel_id=1, source_target_pairs={{0,32},{16,48},{32,0},{48,16},{1,33},{17,49},{33,1},{49,17},{2,34}... | collective-permute-start | bytes 196616 | tf_op jit(solution)/shard_map/ppermute | solution.py:35
  17.4 8.6 %collective-permute-start.2 = (bf16[16,2048]{1,0:T(8,128)(2,1)}, bf16[16,2048]{1,0:T(8,128)(2,1)S(1)}, u32[]{:S(2)}, u32[]{:S(2)}) collective-permute-start(bf16[16,2048]{1,0:T(8,128)(2,1)} %param.9), channel_id=1, source_target_pairs={{0,16},{16,32},{32,48},{48,0},{1,17},{17,33},{33,49},{49,1},{2,18}... | collective-permute-start | bytes 196616 | tf_op jit(solution)/shard_map/ppermute | solution.py:35
  29.2 20.4 %copy-start.6 = (f32[512]{0:T(512)S(1)}, f32[512]{0:T(512)}, u32[]{:S(2)}) copy-start(f32[512]{0:T(512)} %param.8) | copy-start | bytes 6148
  79.0 14.0 %all-to-all-start.2 = ((bf16[16,32,512]{2,1,0:T(8,128)(2,1)}), bf16[16,32,512]{2,1,0:T(8,128)(2,1)S(1)}, u32[]{:S(2)}, u32[]{:S(2)}) async-start(bf16[16,32,512]{2,1,0:T(8,128)(2,1)} %bitcast.42), calls=%async_computation.2 | async-start | bytes 1048576 | tf_op jit(solution)/shard_map/all_to_all | solution.py:25
  84.8 54.9 %reduce-scatter.2.cloned.1.call-start = ((), (), s32[]{:S(2)}) async-start(), calls=%async_computation.9 | async-start | bytes 2359296 | tf_op jit(solution)/shard_map/reduce_scatter | solution.py:75
  88.6 11.9 %copy-start.1 = (bf16[512,448]{0,1:T(8,128)(2,1)S(1)}, bf16[512,448]{0,1:T(8,128)(2,1)}, u32[]{:S(2)}) copy-start(bf16[512,448]{0,1:T(8,128)(2,1)} %param.6) | copy-start | bytes 1376260
  88.6 11.9 %copy-start.4 = (bf16[512,64]{0,1:T(8,128)(2,1)S(1)}, bf16[512,64]{0,1:T(8,128)(2,1)}, u32[]{:S(2)}) copy-start(bf16[512,64]{0,1:T(8,128)(2,1)} %param.11) | copy-start | bytes 196612
  94.4 15.8 %all-to-all-start.3 = ((bf16[16,40,512]{2,1,0:T(8,128)(2,1)}), bf16[16,40,512]{2,1,0:T(8,128)(2,1)S(1)}, u32[]{:S(2)}, u32[]{:S(2)}) async-start(bf16[16,40,512]{2,1,0:T(8,128)(2,1)} %broadcast_in_dim.12), calls=%async_computation.3 | async-start | bytes 1310720 | tf_op jit(solution)/shard_map/all_to_all | solution.py:31
  110.4 0.8 copy-start.2
  111.2 5.1 %copy-start.3 = (bf16[16,32,512]{2,1,0:T(8,128)(2,1)S(1)}, bf16[16,32,512]{2,1,0:T(8,128)(2,1)}, u32[]{:S(2)}) copy-start(bf16[16,32,512]{2,1,0:T(8,128)(2,1)} %copy-done.2) | copy-start | bytes 1572868
  112.0 27.1 %all-to-all-start.4 = ((bf16[8,64,512]{2,1,0:T(8,128)(2,1)}), bf16[8,64,512]{2,1,0:T(8,128)(2,1)S(1)}, u32[]{:S(2)}, u32[]{:S(2)}) async-start(bf16[8,64,512]{2,1,0:T(8,128)(2,1)} %maximum_maximum_fusion), calls=%async_computation.4 | async-start | bytes 1048576 | tf_op jit(solution)/shard_map/all_to_all | solution.py:109
  139.7 23.2 %copy-start.5 = (bf16[64,2048]{1,0:T(8,128)(2,1)S(1)}, bf16[64,2048]{1,0:T(8,128)(2,1)}, u32[]{:S(2)}) copy-start(bf16[64,2048]{1,0:T(8,128)(2,1)} %reduce-scatter.2.cloned.1.call-done) | copy-start | bytes 786436
  158.0 23.3 %all-to-all-start.6 = ((bf16[8,64,512]{2,1,0:T(8,128)(2,1)}), bf16[8,64,512]{2,1,0:T(8,128)(2,1)S(1)}, u32[]{:S(2)}, u32[]{:S(2)}) async-start(bf16[8,64,512]{2,1,0:T(8,128)(2,1)} %broadcast_in_dim.14), calls=%async_computation.7 | async-start | bytes 1048576 | tf_op jit(solution)/shard_map/all_to_all | solution.py:31
  162.9 10.7 %collective-permute-start.5 = (bf16[16,2048]{1,0:T(8,128)(2,1)S(1)}, bf16[16,2048]{1,0:T(8,128)(2,1)S(1)}, u32[]{:S(2)}, u32[]{:S(2)}) collective-permute-start(bf16[16,2048]{1,0:T(8,128)(2,1)S(1)} %get-tuple-element.15), channel_id=1, source_target_pairs={{0,48},{16,0},{32,16},{48,32},{1,49},{17,1},{33,17},{49,33},{2,50}... | collective-permute-start | bytes 196616 | tf_op jit(solution)/shard_map/ppermute | solution.py:35
  165.8 10.2 %collective-permute-start.4 = (bf16[16,2048]{1,0:T(8,128)(2,1)S(1)}, bf16[16,2048]{1,0:T(8,128)(2,1)S(1)}, u32[]{:S(2)}, u32[]{:S(2)}) collective-permute-start(bf16[16,2048]{1,0:T(8,128)(2,1)S(1)} %get-tuple-element.16), channel_id=1, source_target_pairs={{0,32},{16,48},{32,0},{48,16},{1,33},{17,49},{33,1},{49,17},{2,34}... | collective-permute-start | bytes 196616 | tf_op jit(solution)/shard_map/ppermute | solution.py:35
  171.7 9.0 %collective-permute-start.3 = (bf16[16,2048]{1,0:T(8,128)(2,1)S(1)}, bf16[16,2048]{1,0:T(8,128)(2,1)S(1)}, u32[]{:S(2)}, u32[]{:S(2)}) collective-permute-start(bf16[16,2048]{1,0:T(8,128)(2,1)S(1)} %get-tuple-element.14), channel_id=1, source_target_pairs={{0,16},{16,32},{32,48},{48,0},{1,17},{17,33},{33,49},{49,1},{2,18}... | collective-permute-start | bytes 196616 | tf_op jit(solution)/shard_map/ppermute | solution.py:35
Sparse Core Ops, SparseCore 0:
  27.7 47.5 all-gather.1
  88.7 50.8 reduce-scatter.1

commit v4 on v3

--- a/solution.py
+++ b/solution.py
@@ -57,11 +57,7 @@
     n_z, n_yh, n_t = sizes
     lat = norm_gain.shape[0]
     here = lax.axis_index("yh")
-    blocks = [shift(w_up, "yh", n_yh, k) for k in range(1, n_yh)]
-    circle = jnp.concatenate(blocks[::-1] + [w_up] + blocks[::-1], axis=0)
-    w_up_near = lax.dynamic_slice_in_dim(
-        circle, (n_yh - 1 - here) * w_up.shape[0], n_yh * w_up.shape[0], 0
-    )
+    w_up_near = lax.all_gather(w_up, "yh", axis=0, tiled=True)
     w_up_all = lax.all_gather(w_up_near, "z", axis=0, tiled=True)
 
     projected = scatter_sum(

time: 191 us -> 188 us (0.984)
  the two profiles are of different devices: /device:TPU:4 before, /device:TPU:20 now
where the time goes in v4:
time: 188 us; the launch traced here: 187 us
  blocking collectives  66.2 us (35%)
  waiting for transfers between devices  54.1 us (29%)
  starting transfers between devices  33 us (18%)
  between operations  14.3 us (8%)
  matrix products  12 us (6%)
  other arithmetic  3.66 us (2%)
  local copies, waits for them, and re-layouts  3.37 us (2%)
    all_to_all x2, blocking collectives, spread(): return lax.all_to_all(copies, axes, 0, 0, tiled=True)  30.6 us
    all_to_all x1, waiting for transfers between devices, body(): arrived = lax.all_to_all(packed, 'z', 0, 0, tiled=True).astype(jnp.float32)  20.4 us
    all_to_all x1, blocking collectives, scatter_sum(): arrived = lax.all_to_all(pieces, axes, 0, 0, tiled=True)  18.8 us
    all_gather x1, blocking collectives, body(): w_up_near = lax.all_gather(w_up, 'yh', axis=0, tiled=True)  16.8 us
    all_gather x1, waiting for transfers between devices, body(): w_up_all = lax.all_gather(w_up_near, 'z', axis=0, tiled=True)  12.8 us
    ppermute x3, starting transfers between devices, shift(): lax.ppermute(value, axis, [(i, (i + step) % parts) for i in range(parts)])  12.6 us
    dot_general x6, matrix products, dot(): lax.dot_general(a, b, (dims, ((), ())), preferred_element_type=jnp.float32)  12 us
    all_to_all x2, starting transfers between devices, spread(): return lax.all_to_all(copies, axes, 0, 0, tiled=True)  10.2 us
  transfers between devices with their start and end apart: 9, of which 6 were waited for; matrix products, arithmetic and copies ran while one was open for 6% of the time, Pallas kernels for 0%

profile of v4, /device:TPU:20, one launch (start us, length us, event | category | flops | bytes accessed | tf_op | source)
XLA Modules:
  0.0 186.7 jit_solution(17332069848035499525)
XLA Ops:
  7.2 16.8 %all_gather.6 = bf16[64,2048]{1,0:T(8,128)(2,1)} all-gather(bf16[16,2048]{1,0:T(8,128)(2,1)} %param.9), channel_id=1, replica_groups=mesh['z'=8,'yh'=4,'x'=4,'yl'=2,'core'=2] {'yh'}, dimensions={0}, use_global_device_ids=true | all-gather | bytes 327680 | tf_op jit(solution)/shard_map/all_gather | solution.py:60
  24.0 1.6 fusion.4
  25.7 18.8 %all_to_all.35 = f32[16,32,512]{2,1,0:T(8,128)S(1)} all-to-all(f32[16,32,512]{2,1,0:T(8,128)S(1)} %bitcast.37), channel_id=1, replica_groups=mesh['z'=8,'yh'=4,'x'=4,'yl'=2,'core'=2] {'x','yl','core'}, dimensions={0} | all-to-all | bytes 2097152 | tf_op jit(solution)/shard_map/all_to_all | solution.py:25
  44.8 14.1 %all_to_all.36 = bf16[16,32,512]{2,1,0:T(8,128)(2,1)} all-to-all(bf16[16,32,512]{2,1,0:T(8,128)(2,1)S(1)} %broadcast_in_dim.10), channel_id=1, replica_groups=mesh['z'=8,'yh'=4,'x'=4,'yl'=2,'core'=2] {'x','yl','core'}, dimensions={0} | all-to-all | bytes 1048576 | tf_op jit(solution)/shard_map/all_to_all | solution.py:31
  59.0 12.8 %all-gather.2.cloned.1.call-done = bf16[512,2048]{1,0:T(8,128)(2,1)} async-done(((bf16[64,2048]{1,0:T(8,128)(2,1)}), bf16[512,2048]{1,0:T(8,128)(2,1)}) %all-gather.2.cloned.1.call-update) | async-done | bytes 2097168 | tf_op jit(solution)/shard_map/all_gather | solution.py:61
  71.7 3.7 %convolution_convert_fusion.1 = bf16[512,512]{0,1:T(8,128)(2,1)} fusion(bf16[512,2048]{1,0:T(8,128)(2,1)} %all-gather.2.cloned.1.call-done, bf16[512,2048]{1,0:T(8,128)(2,1)S(1)} %copy-done), kind=kOutput, calls=%fused_computation.1 | convolution fusion | flops 1074003968 | bytes 4718592 | tf_op jit(solution)/shard_map/dot_general | solution.py:14
  75.4 6.0 %all-to-all-start.2 = ((bf16[16,32,512]{2,1,0:T(8,128)(2,1)}), bf16[16,32,512]{2,1,0:T(8,128)(2,1)S(1)}, u32[]{:S(2)}, u32[]{:S(2)}) async-start(bf16[16,32,512]{2,1,0:T(8,128)(2,1)} %bitcast.42), calls=%async_computation.2 | async-start | bytes 1048576 | tf_op jit(solution)/shard_map/all_to_all | solution.py:25
  81.6 3.7 %convolution_convert_fusion = bf16[512,2048]{1,0:T(8,128)(2,1)} fusion(bf16[512,512]{1,0:T(8,128)(2,1)} %bitcast.43, bf16[512,2048]{1,0:T(8,128)(2,1)S(1)} %copy-done), kind=kOutput, calls=%fused_computation | convolution fusion | flops 1074790400 | bytes 4718592 | tf_op jit(solution)/shard_map/dot_general | solution.py:14
  85.3 4.5 %all-to-all-done.2 = bf16[16,32,512]{2,1,0:T(8,128)(2,1)S(1)} async-done(((bf16[16,32,512]{2,1,0:T(8,128)(2,1)}), bf16[16,32,512]{2,1,0:T(8,128)(2,1)S(1)}, u32[]{:S(2)}, u32[]{:S(2)}) %all-to-all-start.2) | async-done | bytes 524320 | tf_op jit(solution)/shard_map/all_to_all | solution.py:25
  89.8 0.1 multiply_reduce_fusion.1
  90.1 0.9 broadcast_in_dim.12
  91.0 6.1 %all-to-all-start.3 = ((bf16[16,40,512]{2,1,0:T(8,128)(2,1)}), bf16[16,40,512]{2,1,0:T(8,128)(2,1)S(1)}, u32[]{:S(2)}, u32[]{:S(2)}) async-start(bf16[16,40,512]{2,1,0:T(8,128)(2,1)} %broadcast_in_dim.12), calls=%async_computation.3 | async-start | bytes 1310720 | tf_op jit(solution)/shard_map/all_to_all | solution.py:31
  97.1 0.3 fusion
  97.4 9.4 %all-to-all-done.3 = bf16[16,40,512]{2,1,0:T(8,128)(2,1)S(1)} async-done(((bf16[16,40,512]{2,1,0:T(8,128)(2,1)}), bf16[16,40,512]{2,1,0:T(8,128)(2,1)S(1)}, u32[]{:S(2)}, u32[]{:S(2)}) %all-to-all-start.3) | async-done | bytes 655392 | tf_op jit(solution)/shard_map/all_to_all | solution.py:31
  107.1 0.4 convolution_convert_fusion.2
  107.5 0.3 copy-done.2
  107.8 0.9 maximum_maximum_fusion
  108.7 4.1 %all-to-all-start.4 = ((bf16[8,64,512]{2,1,0:T(8,128)(2,1)}), bf16[8,64,512]{2,1,0:T(8,128)(2,1)S(1)}, u32[]{:S(2)}, u32[]{:S(2)}) async-start(bf16[8,64,512]{2,1,0:T(8,128)(2,1)} %maximum_maximum_fusion), calls=%async_computation.4 | async-start | bytes 1048576 | tf_op jit(solution)/shard_map/all_to_all | solution.py:105
  112.9 2.4 %convolution_convert_fusion.3 = bf16[512,448]{0,1:T(8,128)(2,1)} fusion(bf16[448,576]{1,0:T(8,128)(2,1)} %param.7, bf16[512,64]{1,0:T(8,128)(2,1)S(1)} %copy.22, bf16[512,512]{1,0:T(8,128)(2,1)S(1)} %bitcast.39), kind=kOutput, calls=%fused_computation.3 | convolution fusion | flops 265650176 | bytes 1564672 | tf_op jit(solution)/shard_map/dot_general | solution.py:14
  115.3 20.4 %all-to-all-done.4 = bf16[8,64,512]{2,1,0:T(8,128)(2,1)S(1)} async-done(((bf16[8,64,512]{2,1,0:T(8,128)(2,1)}), bf16[8,64,512]{2,1,0:T(8,128)(2,1)S(1)}, u32[]{:S(2)}, u32[]{:S(2)}) %all-to-all-start.4) | async-done | bytes 524320 | tf_op jit(solution)/shard_map/all_to_all | solution.py:105
  136.0 16.5 %all_to_all.37 = bf16[4,64,512]{2,1,0:T(8,128)(2,1)S(1)} all-to-all(bf16[4,64,512]{2,1,0:T(8,128)(2,1)S(1)} %broadcast_in_dim.13), channel_id=1, replica_groups=mesh['z'=8,'yh'=4,'x'=4,'yl'=2,'core'=2] {'yh'}, dimensions={0} | all-to-all | bytes 524288 | tf_op jit(solution)/shard_map/all_to_all | solution.py:31
  152.7 0.8 broadcast_in_dim.14
  153.6 4.1 %all-to-all-start.6 = ((bf16[8,64,512]{2,1,0:T(8,128)(2,1)}), bf16[8,64,512]{2,1,0:T(8,128)(2,1)S(1)}, u32[]{:S(2)}, u32[]{:S(2)}) async-start(bf16[8,64,512]{2,1,0:T(8,128)(2,1)} %broadcast_in_dim.14), calls=%async_computation.7 | async-start | bytes 1048576 | tf_op jit(solution)/shard_map/all_to_all | solution.py:31
  157.7 2.9 %collective-permute-start = (bf16[16,2048]{1,0:T(8,128)(2,1)S(1)}, bf16[16,2048]{1,0:T(8,128)(2,1)S(1)}, u32[]{:S(2)}, u32[]{:S(2)}) collective-permute-start(bf16[16,2048]{1,0:T(8,128)(2,1)S(1)} %get-tuple-element.14), channel_id=1, source_target_pairs={{0,16},{16,32},{32,48},{48,0},{1,17},{17,33},{33,49},{49,1},{2,18}... | collective-permute-start | bytes 196616 | tf_op jit(solution)/shard_map/ppermute | solution.py:35
  160.5 7.8 %collective-permute-start.1 = (bf16[16,2048]{1,0:T(8,128)(2,1)S(1)}, bf16[16,2048]{1,0:T(8,128)(2,1)S(1)}, u32[]{:S(2)}, u32[]{:S(2)}) collective-permute-start(bf16[16,2048]{1,0:T(8,128)(2,1)S(1)} %get-tuple-element.16), channel_id=1, source_target_pairs={{0,32},{16,48},{32,0},{48,16},{1,33},{17,49},{33,1},{49,17},{2,34}... | collective-permute-start | bytes 196616 | tf_op jit(solution)/shard_map/ppermute | solution.py:35
  168.4 1.9 %collective-permute-start.2 = (bf16[16,2048]{1,0:T(8,128)(2,1)S(1)}, bf16[16,2048]{1,0:T(8,128)(2,1)S(1)}, u32[]{:S(2)}, u32[]{:S(2)}) collective-permute-start(bf16[16,2048]{1,0:T(8,128)(2,1)S(1)} %get-tuple-element.15), channel_id=1, source_target_pairs={{0,48},{16,0},{32,16},{48,32},{1,49},{17,1},{33,17},{49,33},{2,50}... | collective-permute-start | bytes 196616 | tf_op jit(solution)/shard_map/ppermute | solution.py:35
  170.3 0.3 collective-permute-done.1
  170.6 6.7 %collective-permute-done.2 = bf16[16,2048]{1,0:T(8,128)(2,1)S(1)} collective-permute-done((bf16[16,2048]{1,0:T(8,128)(2,1)S(1)}, bf16[16,2048]{1,0:T(8,128)(2,1)S(1)}, u32[]{:S(2)}, u32[]{:S(2)}) %collective-permute-start.2) | collective-permute-done | bytes 65568 | tf_op jit(solution)/shard_map/ppermute | solution.py:35
  177.4 0.7 fusion.8
  178.0 0.1 copy.24
  178.3 0.7 add.72
  179.0 0.9 pad_maximum_fusion
  (59 shorter events, 1.8 us)
Async XLA Ops:
  7.2 64.6 %copy-start = (bf16[512,2048]{1,0:T(8,128)(2,1)S(1)}, bf16[512,2048]{1,0:T(8,128)(2,1)}, u32[]{:S(2)}) copy-start(bf16[512,2048]{1,0:T(8,128)(2,1)} %param.10) | copy-start | bytes 6291460
  7.2 64.6 %all-gather.2.cloned.1.call-start = ((), (), s32[]{:S(2)}) async-start(), calls=%async_computation.8 | async-start | bytes 2359296 | tf_op jit(solution)/shard_map/all_gather | solution.py:61
  25.7 19.0 %copy-start.6 = (f32[512]{0:T(512)S(1)}, f32[512]{0:T(512)}, u32[]{:S(2)}) copy-start(f32[512]{0:T(512)} %param.8) | copy-start | bytes 6148
  75.4 14.3 %all-to-all-start.2 = ((bf16[16,32,512]{2,1,0:T(8,128)(2,1)}), bf16[16,32,512]{2,1,0:T(8,128)(2,1)S(1)}, u32[]{:S(2)}, u32[]{:S(2)}) async-start(bf16[16,32,512]{2,1,0:T(8,128)(2,1)} %bitcast.42), calls=%async_computation.2 | async-start | bytes 1048576 | tf_op jit(solution)/shard_map/all_to_all | solution.py:25
  81.4 54.5 %reduce-scatter.2.cloned.1.call-start = ((), (), s32[]{:S(2)}) async-start(), calls=%async_computation.9 | async-start | bytes 2359296 | tf_op jit(solution)/shard_map/reduce_scatter | solution.py:71
  85.2 11.9 %copy-start.1 = (bf16[512,448]{0,1:T(8,128)(2,1)S(1)}, bf16[512,448]{0,1:T(8,128)(2,1)}, u32[]{:S(2)}) copy-start(bf16[512,448]{0,1:T(8,128)(2,1)} %param.6) | copy-start | bytes 1376260
  85.2 11.9 %copy-start.4 = (bf16[512,64]{0,1:T(8,128)(2,1)S(1)}, bf16[512,64]{0,1:T(8,128)(2,1)}, u32[]{:S(2)}) copy-start(bf16[512,64]{0,1:T(8,128)(2,1)} %param.11) | copy-start | bytes 196612
  91.0 15.8 %all-to-all-start.3 = ((bf16[16,40,512]{2,1,0:T(8,128)(2,1)}), bf16[16,40,512]{2,1,0:T(8,128)(2,1)S(1)}, u32[]{:S(2)}, u32[]{:S(2)}) async-start(bf16[16,40,512]{2,1,0:T(8,128)(2,1)} %broadcast_in_dim.12), calls=%async_computation.3 | async-start | bytes 1310720 | tf_op jit(solution)/shard_map/all_to_all | solution.py:31
  107.0 0.8 copy-start.2
  107.8 5.1 %copy-start.3 = (bf16[16,32,512]{2,1,0:T(8,128)(2,1)S(1)}, bf16[16,32,512]{2,1,0:T(8,128)(2,1)}, u32[]{:S(2)}) copy-start(bf16[16,32,512]{2,1,0:T(8,128)(2,1)} %copy-done.2) | copy-start | bytes 1572868
  108.7 27.0 %all-to-all-start.4 = ((bf16[8,64,512]{2,1,0:T(8,128)(2,1)}), bf16[8,64,512]{2,1,0:T(8,128)(2,1)S(1)}, u32[]{:S(2)}, u32[]{:S(2)}) async-start(bf16[8,64,512]{2,1,0:T(8,128)(2,1)} %maximum_maximum_fusion), calls=%async_computation.4 | async-start | bytes 1048576 | tf_op jit(solution)/shard_map/all_to_all | solution.py:105
  135.9 21.7 %copy-start.5 = (bf16[64,2048]{1,0:T(8,128)(2,1)S(1)}, bf16[64,2048]{1,0:T(8,128)(2,1)}, u32[]{:S(2)}) copy-start(bf16[64,2048]{1,0:T(8,128)(2,1)} %reduce-scatter.2.cloned.1.call-done) | copy-start | bytes 786436
  153.6 24.5 %all-to-all-start.6 = ((bf16[8,64,512]{2,1,0:T(8,128)(2,1)}), bf16[8,64,512]{2,1,0:T(8,128)(2,1)S(1)}, u32[]{:S(2)}, u32[]{:S(2)}) async-start(bf16[8,64,512]{2,1,0:T(8,128)(2,1)} %broadcast_in_dim.14), calls=%async_computation.7 | async-start | bytes 1048576 | tf_op jit(solution)/shard_map/all_to_all | solution.py:31
  157.7 12.6 %collective-permute-start = (bf16[16,2048]{1,0:T(8,128)(2,1)S(1)}, bf16[16,2048]{1,0:T(8,128)(2,1)S(1)}, u32[]{:S(2)}, u32[]{:S(2)}) collective-permute-start(bf16[16,2048]{1,0:T(8,128)(2,1)S(1)} %get-tuple-element.14), channel_id=1, source_target_pairs={{0,16},{16,32},{32,48},{48,0},{1,17},{17,33},{33,49},{49,1},{2,18}... | collective-permute-start | bytes 196616 | tf_op jit(solution)/shard_map/ppermute | solution.py:35
  160.5 10.1 %collective-permute-start.1 = (bf16[16,2048]{1,0:T(8,128)(2,1)S(1)}, bf16[16,2048]{1,0:T(8,128)(2,1)S(1)}, u32[]{:S(2)}, u32[]{:S(2)}) collective-permute-start(bf16[16,2048]{1,0:T(8,128)(2,1)S(1)} %get-tuple-element.16), channel_id=1, source_target_pairs={{0,32},{16,48},{32,0},{48,16},{1,33},{17,49},{33,1},{49,17},{2,34}... | collective-permute-start | bytes 196616 | tf_op jit(solution)/shard_map/ppermute | solution.py:35
  168.4 9.0 %collective-permute-start.2 = (bf16[16,2048]{1,0:T(8,128)(2,1)S(1)}, bf16[16,2048]{1,0:T(8,128)(2,1)S(1)}, u32[]{:S(2)}, u32[]{:S(2)}) collective-permute-start(bf16[16,2048]{1,0:T(8,128)(2,1)S(1)} %get-tuple-element.15), channel_id=1, source_target_pairs={{0,48},{16,0},{32,16},{48,32},{1,49},{17,1},{33,17},{49,33},{2,50}... | collective-permute-start | bytes 196616 | tf_op jit(solution)/shard_map/ppermute | solution.py:35
Sparse Core Ops, SparseCore 0:
  24.2 47.5 all-gather.1
  85.4 50.4 reduce-scatter.1
